TPU v7x, 512 devices: a whole 4x4x16 slice. The times are simulated.
512 devices in a mesh: tm: 64 (over x, z), space: 8 (over y, core).
Axes of the slice: x: 4, y: 4, z: 16, core: 2. Of those that a mesh axis runs over, the one named last changes fastest.
Arguments:
- traj: float32 [64, 32, 128, 128], P('tm', None, 'space'), may hold values from -6 to 6
- start_state: float32 [32, 128, 128], P(None, 'space'), may hold values from -6 to 6
- actions: float32 [64, 16], P('tm'), may hold values from -6 to 6
- hidden_w: bfloat16 [3, 9, 32, 32], replicated, may hold values from -0.375 to 0.375
- hidden_b: float32 [3, 32], replicated, may hold values from -3 to 3
- head_w: bfloat16 [9, 64, 32], replicated, may hold values from -0.375 to 0.375
- cand_b: float32 [32], replicated, may hold values from -3 to 3
- gate_b: float32 [32], replicated, may hold values from 0 to 9
- skip: float32 [32], replicated, may hold values from 0.1 to 0.9
- act_proj: float32 [16, 64], replicated, may hold values from -1.5 to 1.5
Outputs:
- new_traj: float32 [64, 32, 128, 128], P('tm', None, 'space')
- res_msq: float32 [64], P('tm')
All inputs are finite; a program needn't handle non-finite values.
Results may differ from a plain program's by a relative error of at most 0.0015.
Values may be sent and summed in bfloat16 or wider, within the bound.
No kernel may reach another device: no remote copies, remote signals or barrier semaphores. Data moves between devices by JAX's collectives and lax.ppermute only.
A program may use at most 128 MiB of HBM per device.

v0:
```python
import jax
import jax.numpy as jnp
from jax import lax
from jax.sharding import PartitionSpec as P


def extended_2(block, sides, width):
    for axis, dim in sides:
        count = lax.axis_size(axis)
        forward = [(i, i + 1) for i in range(count - 1)]
        backward = [(target, source) for source, target in forward]
        low = lax.ppermute(
            lax.slice_in_dim(block, block.shape[dim] - width, None, axis=dim), axis, forward
        )
        high = lax.ppermute(lax.slice_in_dim(block, 0, width, axis=dim), axis, backward)
        block = jnp.concatenate([low, block, high], axis=dim)
    return block


def from_behind(value, axis, by):
    length = lax.axis_size(axis)
    pairs = [(i, i + by) for i in range(length) if 0 <= i + by < length]
    return lax.ppermute(value, axis, pairs)


def entering(part, axis, combine, identity):
    place = lax.axis_index(axis)
    gathered = jax.tree.map(lambda a: lax.all_gather(a, axis), part)
    state = jax.tree.map(lambda a, e: jnp.zeros_like(a) + jnp.asarray(e, a.dtype), part, identity)

    def one(step, state):
        return combine(
            state, jax.tree.map(lambda a: lax.dynamic_index_in_dim(a, step, 0, False), gathered)
        )

    return lax.fori_loop(0, place, one, state)


def conv_rows(extended, taps):
    rows_out = extended.shape[2] - 2
    width = extended.shape[3]
    padded = jnp.pad(extended, ((0, 0), (0, 0), (0, 0), (1, 1)))
    total = None
    for offa in range(3):
        for offb in range(3):
            term = jnp.einsum(
                "oc,schw->sohw",
                taps[offa * 3 + offb],
                padded[:, :, offa : offa + rows_out, offb : offb + width],
                preferred_element_type=jnp.float32,
            )
            total = term if total is None else total + term
    return total


def rim_rows(hidden):
    return extended_2(hidden, (("space", 2),), 1)


def combine(earlier, later):
    return (later[0] * earlier[0], later[0] * earlier[1] + later[1])


def body(traj, start_state, actions, hidden_w, hidden_b, head_w, cand_b, gate_b, skip, act_proj):
    steps, chans, strip_rows, width = traj.shape
    prior = from_behind(traj[steps - 1].astype(jnp.bfloat16), "tm", 1).astype(jnp.float32)
    first = jnp.where(lax.axis_index("tm") == 0, start_state, prior)
    guess_in = jnp.concatenate([first[None], traj[: steps - 1]], axis=0)
    act_terms = jnp.dot(
        actions, act_proj, precision=lax.Precision.HIGHEST, preferred_element_type=jnp.float32
    )
    hidden = guess_in.astype(jnp.bfloat16)
    layers = hidden_w.shape[0]
    for layer in range(layers):
        pre = conv_rows(rim_rows(hidden), hidden_w[layer]) + hidden_b[layer][None, :, None, None]
        if layer == 0:
            pre = pre + act_terms[:, :chans, None, None]
        hidden = jax.nn.silu(pre).astype(jnp.bfloat16)
    head = conv_rows(rim_rows(hidden), head_w)
    cand = jnp.tanh(
        head[:, :chans] + cand_b[None, :, None, None] + skip[None, :, None, None] * guess_in
    )
    gate = jax.nn.sigmoid(
        head[:, chans:] + gate_b[None, :, None, None] + act_terms[:, chans:, None, None]
    )
    fval = gate * guess_in + (1.0 - gate) * cand
    jac = gate + (1.0 - gate) * (1.0 - cand * cand) * skip[None, :, None, None]
    local_sq = jnp.sum((traj - fval) ** 2, axis=(1, 2, 3))
    total_sq = lax.psum(local_sq, "space")
    res_msq = total_sq / (chans * strip_rows * width * lax.axis_size("space"))
    offs = fval - jac * guess_in

    def compose(carry, pair):
        return ((pair[0] * carry[0], pair[0] * carry[1] + pair[1]), None)

    ones = jnp.ones_like(start_state)
    zeros = jnp.zeros_like(start_state)
    (block_a, block_b), _ = lax.scan(compose, (ones, zeros), (jac, offs))
    prefix_a, prefix_b = entering((block_a, block_b), "tm", combine, (ones, zeros))
    state = prefix_a * start_state + prefix_b

    def advance(yval, pair):
        nxt = pair[0] * yval + pair[1]
        return (nxt, nxt)

    _, new_traj = lax.scan(advance, state, (jac, offs))
    return (new_traj, res_msq)


def solution(mesh):
    return jax.shard_map(
        body,
        mesh=mesh,
        in_specs=(
            P("tm", None, "space", None),
            P(None, "space", None),
            P("tm", None),
            P(),
            P(),
            P(),
            P(),
            P(),
            P(),
            P(),
        ),
        out_specs=(P("tm", None, "space", None), P("tm")),
        check_vma=False,
    )
```

profile of v0, /device:TPU:486, one launch (start us, length us, event | category | flops | bytes accessed | tf_op | source)
XLA Modules:
  0.0 542.2 jit_solution(13539159868623416270)
XLA Ops:
  8.4 1.3 collective-permute-start
  11.3 4.2 collective-permute-done
  16.6 1.3 collective-permute-start.1
  17.9 1.3 collective-permute-start.2
  19.3 3.5 collective-permute-done.2
  31.4 4.3 collective-permute-start.3
  35.7 1.3 collective-permute-start.4
  37.0 1.8 collective-permute-done.4
  47.0 3.9 collective-permute-start.5
  50.9 1.3 collective-permute-start.6
  52.2 1.8 collective-permute-done.6
  62.2 3.8 collective-permute-start.7
  66.0 1.3 collective-permute-start.8
  67.3 1.8 collective-permute-done.8
  75.0 15.0 %psum.7 = f32[1]{0:T(128)} all-reduce(f32[1]{0:T(128)} %bitcast.133), channel_id=1, replica_groups=mesh['tm'=64,'space'=8] {'space'}, use_global_device_ids=true, to_apply=%region_3.4 | all-reduce | flops 1 | bytes 8 | tf_op jit(solution)/shard_map/psum | solution.py:89
  90.6 173.3 %all-gather.5.cloned.1.call-done = f32[64,32,16,128]{3,2,1,0:T(8,128)} async-done(((f32[1,32,16,128]{3,2,1,0:T(8,128)}), f32[64,32,16,128]{3,2,1,0:T(8,128)}) %all-gather.5.cloned.1.call-update) | async-done | bytes 16777232 | tf_op jit(solution)/shard_map/all_gather | solution.py:28
  263.9 192.8 %all-gather.3.cloned.1.call-done = f32[64,32,16,128]{3,2,1,0:T(8,128)} async-done(((f32[1,32,16,128]{3,2,1,0:T(8,128)}), f32[64,32,16,128]{3,2,1,0:T(8,128)}) %all-gather.3.cloned.1.call-update) | async-done | bytes 16777232 | tf_op jit(solution)/shard_map/all_gather | solution.py:28
  456.8 76.3 %while.2 = (s32[]{:T(128)}, f32[32,16,128]{2,1,0:T(8,128)S(1)}, f32[32,16,128]{2,1,0:T(8,128)S(1)}, s32[]{:T(128)}, f32[64,32,16,128]{3,2,1,0:T(8,128)}, /*index...) while((s32[]{:T(128)}, f32[32,16,128]{2,1,0:T(8,128)S(1)}, f32[32,16,128]{2,1,0:T(8,128)S(1)}, ...), condition=%wide.region_1.2_spmd, body=%wide.region_0.1_spmd.sunk | while | flops 196613 | bytes 1573003 | solution.py:36
  456.8 1.2 bitcast_add_fusion.3
  458.0 1.2 bitcast_add_fusion.3
  459.2 1.2 bitcast_add_fusion.3
  460.4 1.2 bitcast_add_fusion.3
  461.6 1.2 bitcast_add_fusion.3
  462.8 1.2 bitcast_add_fusion.3
  (136 shorter events, 103.5 us)
Async XLA Ops:
  7.2 2.5 copy-start
  7.2 64.7 %copy-start.2 = (f32[1,32,16,128]{3,2,1,0:T(8,128)S(1)}, f32[1,32,16,128]{3,2,1,0:T(8,128)}, u32[]{:S(2)}) copy-start(f32[1,32,16,128]{3,2,1,0:T(8,128)} %param.12) | copy-start | bytes 786436
  7.2 64.7 %copy-start.1 = (f32[32,16,128]{2,1,0:T(8,128)S(1)}, f32[32,16,128]{2,1,0:T(8,128)}, u32[]{:S(2)}) copy-start(f32[32,16,128]{2,1,0:T(8,128)} %param.13) | copy-start | bytes 786436
  7.2 62.1 %copy-start.3 = (bf16[9,64,32]{1,2,0:T(8,128)(2,1)S(1)}, bf16[9,64,32]{1,2,0:T(8,128)(2,1)}, u32[]{:S(2)}) copy-start(bf16[9,64,32]{1,2,0:T(8,128)(2,1)} %param.17) | copy-start | bytes 110596
  7.2 64.7 %copy-start.4 = (f32[32]{0:T(128)S(1)}, f32[32]{0:T(128)}, u32[]{:S(2)}) copy-start(f32[32]{0:T(128)} %param.20) | copy-start | bytes 388
  7.2 64.7 %copy-start.6 = (f32[32]{0:T(128)S(1)}, f32[32]{0:T(128)}, u32[]{:S(2)}) copy-start(f32[32]{0:T(128)} %param.19) | copy-start | bytes 388
  7.2 64.7 %copy-start.5 = (f32[32]{0:T(128)S(1)}, f32[32]{0:T(128)}, u32[]{:S(2)}) copy-start(f32[32]{0:T(128)} %param.18) | copy-start | bytes 388
  7.2 256.7 %all-gather.5.cloned.1.call-start = ((), (), s32[]{:S(2)}) async-start(), calls=%async_computation.1 | async-start | bytes 17039360 | tf_op jit(solution)/shard_map/all_gather | solution.py:28
  8.4 7.1 %collective-permute-start = (bf16[32,16,128]{2,0,1:T(8,128)(2,1)S(1)}, bf16[32,16,128]{2,0,1:T(8,128)(2,1)S(1)}, u32[]{:S(2)}, u32[]{:S(2)}) collective-permute-start(bf16[32,16,128]{2,0,1:T(8,128)(2,1)S(1)} %bitcast.381), channel_id=1, source_target_pairs={{0,8},{8,16},{16,24},{24,32},{32,40},{40,48},{48,56},{56,64},{64,7... | collective-permute-start | bytes 393224 | tf_op jit(solution)/shard_map/ppermute | solution.py:23
  16.6 2.7 collective-permute-start.1
  17.9 4.9 collective-permute-start.2
  31.4 5.6 %collective-permute-start.3 = (bf16[1,32,1,128]{3,1,2,0:T(8,128)(2,1)S(1)}, bf16[1,32,1,128]{3,1,2,0:T(8,128)(2,1)S(1)}, u32[]{:S(2)}, u32[]{:S(2)}) collective-permute-start(bf16[1,32,1,128]{3,1,2,0:T(8,128)(2,1)S(1)} %get-tuple-element.100), channel_id=1, source_target_pairs={{0,1},{1,2},{2,3},{3,4},{4,5},{5,6},{6,7},{8,9},{9,10},{10,11},{11... | collective-permute-start | bytes 24584 | tf_op jit(solution)/shard_map/ppermute | solution.py:12
  35.7 3.1 collective-permute-start.4
  47.0 5.2 collective-permute-start.5
  50.9 3.1 collective-permute-start.6
  62.2 5.2 collective-permute-start.7
  66.0 3.1 collective-permute-start.8
  74.0 382.7 %all-gather.3.cloned.1.call-start = ((), (), s32[]{:S(2)}) async-start(), calls=%async_computation | async-start | bytes 17039360 | tf_op jit(solution)/shard_map/all_gather | solution.py:28
Sparse Core Ops, SparseCore 0:
  74.1 189.7 all-gather.4
  267.5 189.2 all-gather.2
where the time goes:
time: 545 us; the launch traced here: 542 us
  waiting for transfers between devices  379 us (70%)
  other arithmetic  78.1 us (14%)
  matrix products  27.7 us (5%)
  starting transfers between devices  19.8 us (4%)
  between operations  16.4 us (3%)
  blocking collectives  15 us (3%)
    all_gather x2, waiting for transfers between devices, entering(): gathered = jax.tree.map(lambda a: lax.all_gather(a, axis), part)  366 us
    add x63, other arithmetic, combine(): return (later[0] * earlier[0], later[0] * earlier[1] + later[1])  75 us
    dot_general x36, matrix products, conv_rows(): jnp.einsum('oc,schw->sohw', taps[offa * 3 + offb], padded[:, :, offa:offa...  26.9 us
    psum x1, blocking collectives, body(): total_sq = lax.psum(local_sq, 'space')  15 us
    ppermute x4, starting transfers between devices, extended_2(): lax.ppermute(lax.slice_in_dim(block, block.shape[dim] - width, None, axis...  13.3 us
  transfers between devices with their start and end apart: 11, of which 7 were waited for; matrix products, arithmetic and copies ran while one was open for 0% of the time, Pallas kernels for 0%

commit v1 on v0

v1 whole, which is shorter than its diff:
```python
import jax
import jax.numpy as jnp
from jax import lax
from jax.experimental import pallas as pl
from jax.experimental.pallas import tpu as pltpu
from jax.sharding import PartitionSpec as P

NX = 4
NZ = 16
HALO = 4
GROUP = 6


def column(vec):
    n = vec.shape[1]
    rows = lax.broadcasted_iota(jnp.int32, (n, n), 0)
    cols = lax.broadcasted_iota(jnp.int32, (n, n), 1)
    return jnp.sum(jnp.where(rows == cols, jnp.broadcast_to(vec, (n, n)), 0.0), axis=1, keepdims=True)


def groups_of(rows):
    return [(g, min(GROUP, rows - g)) for g in range(0, rows, GROUP)]


def conv_kernel(
    main_ref, low_ref, high_ref, traj_ref, act_ref, proj_ref, wh_ref, hb_ref, wo_ref, cb_ref, gb_ref, sk_ref,
    maps_ref, res_ref, xa_ref, xb_ref, band_ref, head_ref,
):
    strip = lax.axis_index("space")
    width = main_ref.shape[2]
    chans = main_ref.shape[1]
    rows = main_ref.shape[0]
    lanes = lax.broadcasted_iota(jnp.int32, (chans, width), 1)
    first, last = lanes == 0, lanes == width - 1

    for ref in (xa_ref, xb_ref):
        ref[:, 3 * chans :, :] = jnp.zeros((ref.shape[0], ref.shape[1] - 3 * chans, width), jnp.bfloat16)
    band_ref[...] = jnp.zeros(band_ref.shape, jnp.bfloat16)
    head_ref[...] = jnp.zeros(head_ref.shape, jnp.bfloat16)

    act = column(act_ref[...])
    terms = jnp.sum(act * proj_ref[...], axis=0, keepdims=True)
    biases = [column(hb_ref[l : l + 1, :]) for l in range(3)]
    biases[0] = biases[0] + column(terms[:, :chans])
    gate_bias = column(gb_ref[...]) + column(terms[:, chans:])
    cand_bias = column(cb_ref[...])
    skip = column(sk_ref[...])

    def put(ref, row, value):
        ref[row, :chans, :] = jnp.where(first, 0.0, pltpu.roll(value, 1, 1)).astype(jnp.bfloat16)
        ref[row, chans : 2 * chans, :] = value.astype(jnp.bfloat16)
        ref[row, 2 * chans : 3 * chans, :] = jnp.where(last, 0.0, pltpu.roll(value, width - 1, 1)).astype(jnp.bfloat16)

    for r in range(HALO):
        put(xa_ref, r, low_ref[r].astype(jnp.float32))
        put(xa_ref, HALO + rows + r, high_ref[r].astype(jnp.float32))
    for r in range(rows):
        put(xa_ref, HALO + r, main_ref[r].astype(jnp.float32))

    def product(band, outs, src, g, n):
        k = (n + 2) * 128
        rhs = src[g : g + n + 2].reshape(k, width)
        return jnp.dot(band[: n * outs, :k], rhs, preferred_element_type=jnp.float32)

    top = strip == 0
    bottom = strip == lax.axis_size("space") - 1
    src, dst = xa_ref, xb_ref
    for layer in range(3):
        for r in range(GROUP):
            for a in range(3):
                band_ref[r * chans : (r + 1) * chans, (r + a) * 128 : (r + a + 1) * 128] = wh_ref[layer, a]
        halo = HALO - 1 - layer
        for g, n in groups_of(rows + 2 * halo):
            acc = product(band_ref, chans, src, g, n).reshape(n, chans, width)
            for j in range(n):
                pre = acc[j] + biases[layer]
                value = 0.5 * pre * (1.0 + jnp.tanh(0.5 * pre))
                if g + j < halo:
                    value = jnp.where(top, 0.0, value)
                if g + j >= halo + rows:
                    value = jnp.where(bottom, 0.0, value)
                put(dst, g + j, value)
        src, dst = dst, src

    for r in range(GROUP):
        for a in range(3):
            head_ref[r * 2 * chans : (r + 1) * 2 * chans, (r + a) * 128 : (r + a + 1) * 128] = wo_ref[a]
    total = jnp.zeros((chans, width), jnp.float32)
    for g, n in groups_of(rows):
        acc = product(head_ref, 2 * chans, src, g, n).reshape(n, 2 * chans, width)
        for j in range(n):
            row = g + j
            guess = main_ref[row].astype(jnp.float32)
            cand = jnp.tanh(acc[j, :chans] + cand_bias + skip * guess)
            rest = 1.0 / (1.0 + jnp.exp(acc[j, chans:] + gate_bias))
            slope = (1.0 - cand * cand) * skip
            maps_ref[row, 0] = rest * (1.0 - slope)
            maps_ref[row, 1] = rest * (cand - slope * guess)
            fval = guess + rest * (cand - guess)
            diff = traj_ref[pl.ds(row, chans, stride=rows), :] - fval
            total = total + diff * diff
    res_ref[...] = jnp.sum(total, axis=0, keepdims=True)


def tap_rows(weights, outs):
    lead = weights.shape[:-3]
    chans = weights.shape[-1]
    split = weights.reshape(lead + (3, 3, outs, chans))
    moved = jnp.swapaxes(split, -3, -2).reshape(lead + (3, outs, 3 * chans))
    return jnp.pad(moved, [(0, 0)] * (len(lead) + 2) + [(0, 128 - 3 * chans)])


def body(traj, start_state, actions, hidden_w, hidden_b, head_w, cand_b, gate_b, skip, act_proj):
    _, chans, rows, width = traj.shape
    n_tm, n_space = lax.axis_size("tm"), lax.axis_size("space")
    place = lax.axis_index("tm")
    source = jnp.where(place == n_tm - 1, start_state, traj[0])
    source = jnp.swapaxes(source.astype(jnp.bfloat16), 0, 1)

    def shifted(value, step):
        pairs = [
            (t * n_space + s, (t + 1) % n_tm * n_space + s + step)
            for t in range(n_tm)
            for s in range(n_space)
            if 0 <= s + step < n_space
        ]
        return lax.ppermute(value, ("tm", "space"), pairs)

    main = shifted(source, 0)
    low = shifted(source[rows - HALO :], 1)
    high = shifted(source[:HALO], -1)

    kb = (GROUP + 2) * 128
    maps, partial = pl.pallas_call(
        conv_kernel,
        out_shape=(
            jax.ShapeDtypeStruct((rows, 2, chans, width), jnp.float32),
            jax.ShapeDtypeStruct((1, width), jnp.float32),
        ),
        scratch_shapes=[
            pltpu.VMEM((rows + 2 * HALO, 128, width), jnp.bfloat16),
            pltpu.VMEM((rows + 2 * HALO, 128, width), jnp.bfloat16),
            pltpu.VMEM((GROUP * chans, kb), jnp.bfloat16),
            pltpu.VMEM((GROUP * 2 * chans, kb), jnp.bfloat16),
        ],
        name="dynamics",
    )(
        main, low, high, traj.reshape(chans * rows, width), actions, act_proj,
        tap_rows(hidden_w, chans), hidden_b, tap_rows(head_w, 2 * chans),
        cand_b[None], gate_b[None], skip[None],
    )

    z_groups = [[x * NZ + z for z in range(NZ)] for x in range(NX)]
    x_groups = [[x * NZ + z for x in range(NX)] for z in range(NZ)]
    sent = lax.all_to_all(maps.astype(jnp.float16), "tm", 0, 0, axis_index_groups=z_groups)
    steps = [(1.0 - sent[z, 0].astype(jnp.float32), sent[z, 1].astype(jnp.float32)) for z in range(NZ)]
    block_a, block_b = steps[0]
    for a, b in steps[1:]:
        block_a, block_b = a * block_a, a * block_b + b
    block = jnp.stack([block_a, block_b])
    blocks = lax.all_to_all(
        jnp.broadcast_to(block[None], (NX,) + block.shape), "tm", 0, 0, axis_index_groups=x_groups
    )
    mine = place // NZ
    state = lax.dynamic_index_in_dim(start_state, place % NZ, 1, False)
    for x in range(NX - 1):
        state = jnp.where(x < mine, blocks[x, 0] * state + blocks[x, 1], state)
    states = []
    for a, b in steps:
        states.append(state)
        state = a * state + b
    back = lax.all_to_all(
        jnp.stack(states).astype(jnp.float16), "tm", 0, 0, axis_index_groups=z_groups
    ).astype(jnp.float32)
    new = back - maps[:, 0] * back + maps[:, 1]
    new_traj = jnp.swapaxes(new, 0, 1)[None]

    parts = lax.all_to_all(jnp.broadcast_to(partial[None], (n_space, 1, width)), "space", 0, 0)
    res_msq = jnp.sum(parts).reshape(1) / (chans * rows * width * n_space)
    return new_traj, res_msq


def solution(mesh):
    return jax.shard_map(
        body,
        mesh=mesh,
        in_specs=(
            P("tm", None, "space", None),
            P(None, "space", None),
            P("tm", None),
            P(),
            P(),
            P(),
            P(),
            P(),
            P(),
            P(),
        ),
        out_specs=(P("tm", None, "space", None), P("tm")),
        check_vma=False,
    )
```

time: 545 us -> 117 us (0.21)
  the two profiles are of different devices: /device:TPU:486 before, /device:TPU:8 now
where the time goes in v1:
time: 117 us; the launch traced here: 115 us
  waiting for transfers between devices  42.4 us (36%)
  starting transfers between devices  35.7 us (31%)
  other arithmetic  24.5 us (21%)
  local copies, waits for them, and re-layouts  6.05 us (5%)
  Pallas kernels  3.99 us (3%)
  between operations  2.6 us (2%)
    unnamed x15, other arithmetic  19.4 us
    all_to_all x1, waiting for transfers between devices, body(): lax.all_to_all(maps.astype(jnp.float16), 'tm', 0, 0, axis_index_groups=z_...  18.5 us
    all_to_all x1, waiting for transfers between devices, body(): lax.all_to_all(jnp.stack(states).astype(jnp.float16), 'tm', 0, 0, axis_in...  13.4 us
    ppermute x3, starting transfers between devices, shifted(): return lax.ppermute(value, ('tm', 'space'), pairs)  11.3 us
    all_to_all x1, starting transfers between devices, body(): lax.all_to_all(maps.astype(jnp.float16), 'tm', 0, 0, axis_index_groups=z_...  9.19 us
    all_to_all x1, starting transfers between devices, body(): lax.all_to_all(jnp.stack(states).astype(jnp.float16), 'tm', 0, 0, axis_in...  5.96 us
    ppermute x3, waiting for transfers between devices, shifted(): return lax.ppermute(value, ('tm', 'space'), pairs)  5.42 us
    all_to_all x1, waiting for transfers between devices, body(): lax.all_to_all(jnp.broadcast_to(block[None], (NX,) + block.shape), 'tm',...  5.06 us
  transfers between devices with their start and end apart: 7, of which 5 were waited for; matrix products, arithmetic and copies ran while one was open for 21% of the time, Pallas kernels for 0%

profile of v1, /device:TPU:8, one launch (start us, length us, event | category | flops | bytes accessed | tf_op | source)
XLA Modules:
  0.0 115.3 jit_solution(3830678799561920503)
XLA Ops:
  1.9 4.0 %collective-permute-start = (bf16[16,32,128]{2,1,0:T(8,128)(2,1)S(1)}, bf16[16,32,128]{2,1,0:T(8,128)(2,1)S(1)}, u32[]{:S(2)}, u32[]{:S(2)}) collective-permute-start(bf16[16,32,128]{2,1,0:T(8,128)(2,1)S(1)} %fusion.3), channel_id=1, source_target_pairs={{0,8},{1,9},{2,10},{3,11},{4,12},{5,13},{6,14},{7,15},{8,16},{9,17... | collective-permute-start | bytes 393224 | tf_op jit(solution)/shard_map/ppermute | solution.py:127
  5.9 2.9 %collective-permute-start.2 = (bf16[4,32,128]{2,1,0:T(8,128)(2,1)S(1)}, bf16[4,32,128]{2,1,0:T(8,128)(2,1)S(1)}, u32[]{:S(2)}, u32[]{:S(2)}) collective-permute-start(bf16[4,32,128]{2,1,0:T(8,128)(2,1)S(1)} %get-tuple-element.28), channel_id=1, source_target_pairs={{1,8},{2,9},{3,10},{4,11},{5,12},{6,13},{7,14},{9,16},{10,17},{11,... | collective-permute-start | bytes 98312 | tf_op jit(solution)/shard_map/ppermute | solution.py:127
  8.7 4.5 %collective-permute-start.1 = (bf16[4,32,128]{2,1,0:T(8,128)(2,1)S(1)}, bf16[4,32,128]{2,1,0:T(8,128)(2,1)S(1)}, u32[]{:S(2)}, u32[]{:S(2)}) collective-permute-start(bf16[4,32,128]{2,1,0:T(8,128)(2,1)S(1)} %get-tuple-element.29), channel_id=1, source_target_pairs={{0,9},{1,10},{2,11},{3,12},{4,13},{5,14},{6,15},{8,17},{9,18},{10,... | collective-permute-start | bytes 98312 | tf_op jit(solution)/shard_map/ppermute | solution.py:127
  15.0 4.0 %collective-permute-done.2.high_ref = bf16[4,32,128]{2,1,0:T(8,128)(2,1)S(1)} collective-permute-done((bf16[4,32,128]{2,1,0:T(8,128)(2,1)S(1)}, bf16[4,32,128]{2,1,0:T(8,128)(2,1)S(1)}, u32[]{:S(2)}, u32[]{:S(2)}) %collective-permute-start.2) | collective-permute-done | bytes 32800 | tf_op jit(solution)/shard_map/ppermute | solution.py:127
  18.9 1.5 %collective-permute-done.1.low_ref = bf16[4,32,128]{2,1,0:T(8,128)(2,1)S(1)} collective-permute-done((bf16[4,32,128]{2,1,0:T(8,128)(2,1)S(1)}, bf16[4,32,128]{2,1,0:T(8,128)(2,1)S(1)}, u32[]{:S(2)}, u32[]{:S(2)}) %collective-permute-start.1) | collective-permute-done | bytes 32800 | tf_op jit(solution)/shard_map/ppermute | solution.py:127
  21.1 4.0 %dynamics.1 = (f32[16,2,32,128]{3,2,1,0:T(8,128)}, f32[1,128]{1,0:T(1,128)}) custom-call(bf16[16,32,128]{2,1,0:T(8,128)(2,1)} %copy-done.3, bf16[4,32,128]{2,1,0:T(8,128)(2,1)} %copy-done.6, bf16[4,32,128]{2,1,0:T(8,128)(2,1)} %copy-done.5, f32[512,128]{1,0:T(8,128)} %bitcast.422, f32[1,16]{1,0:T(1,128)} %act_ref.1, f32[16,64]{1,0:T(8,128)} %proj_ref.1, ...), custom_call_target="tpu_custom_call" | custom-call | tf_op jit(solution)/shard_map/dynamics/pallas_call | solution.py:134
  25.0 1.8 %convert_element_type.1419 = f16[16,2,32,128]{3,2,1,0:T(8,128)(2,1)} convert(f32[16,2,32,128]{3,2,1,0:T(8,128)} %get-tuple-element.4) | non-fusion elementwise | flops 131072 | bytes 786432 | tf_op jit(solution)/shard_map/convert_element_type | solution.py:155
  26.8 9.2 %all-to-all-start = ((f16[16,2,32,128]{3,2,1,0:T(8,128)(2,1)}), f16[16,2,32,128]{3,2,1,0:T(8,128)(2,1)S(1)}, u32[]{:S(2)}, u32[]{:S(2)}) async-start(f16[16,2,32,128]{3,2,1,0:T(8,128)(2,1)} %convert_element_type.1419), calls=%async_computation | async-start | bytes 524288 | tf_op jit(solution)/shard_map/all_to_all | solution.py:155
  36.1 18.5 %all-to-all-done = f16[16,2,32,128]{3,2,1,0:T(8,128)(2,1)S(1)} async-done(((f16[16,2,32,128]{3,2,1,0:T(8,128)(2,1)}), f16[16,2,32,128]{3,2,1,0:T(8,128)(2,1)S(1)}, u32[]{:S(2)}, u32[]{:S(2)}) %all-to-all-start) | async-done | bytes 262176 | tf_op jit(solution)/shard_map/all_to_all | solution.py:155
  55.4 4.3 %all-to-all-start.1 = ((f32[4,2,32,128]{3,2,1,0:T(8,128)}), f32[4,2,32,128]{3,2,1,0:T(8,128)S(1)}, u32[]{:S(2)}, u32[]{:S(2)}) async-start(f32[4,2,32,128]{3,2,1,0:T(8,128)} %broadcast_in_dim.29), calls=%async_computation.1 | async-start | bytes 262144 | tf_op jit(solution)/shard_map/all_to_all | solution.py:161
  60.6 5.1 %all-to-all-done.1 = f32[4,2,32,128]{3,2,1,0:T(8,128)S(1)} async-done(((f32[4,2,32,128]{3,2,1,0:T(8,128)}), f32[4,2,32,128]{3,2,1,0:T(8,128)S(1)}, u32[]{:S(2)}, u32[]{:S(2)}) %all-to-all-start.1) | async-done | bytes 131104 | tf_op jit(solution)/shard_map/all_to_all | solution.py:161
  66.9 4.9 %all-to-all-start.3 = ((f32[8,1,128]{2,1,0:T(1,128)}), f32[8,1,128]{2,1,0:T(1,128)S(1)}, u32[]{:S(2)}, u32[]{:S(2)}) async-start(f32[8,1,128]{2,1,0:T(1,128)} %broadcast_in_dim.32), calls=%async_computation.3 | async-start | bytes 8192 | tf_op jit(solution)/shard_map/all_to_all | solution.py:178
  73.7 1.4 %constant_dynamic-update-slice_fusion.13 = (f16[16,32,128]{2,1,0:T(8,128)(2,1)}, f32[1,32,128]{2,1,0:T(8,128)S(1)}) fusion(f16[16,32,128]{2,1,0:T(8,128)(2,1)} %constant_dynamic-update-slice_fusion.14, f16[16,2,32,128]{3,2,1,0:T(8,128)(2,1)} %copy-done, f32[1,32,128]{2,1,0:T(8,128)S(1)} %get-tuple-element.27), kind=kLoop, calls=%fused_computation.21 | loop fusion | flops 45056 | bytes 73728
  75.1 1.4 %constant_dynamic-update-slice_fusion.12 = f16[16,32,128]{2,1,0:T(8,128)(2,1)} fusion(f16[16,32,128]{2,1,0:T(8,128)(2,1)} %get-tuple-element.24, f16[16,2,32,128]{3,2,1,0:T(8,128)(2,1)} %copy-done, f32[1,32,128]{2,1,0:T(8,128)S(1)} %get-tuple-element.25), kind=kLoop, calls=%fused_computation.20 | loop fusion | flops 24576 | bytes 40960
  76.4 1.3 %constant_dynamic-update-slice_fusion.11 = (f16[16,32,128]{2,1,0:T(8,128)(2,1)}, f32[1,32,128]{2,1,0:T(8,128)S(1)}) fusion(f16[16,32,128]{2,1,0:T(8,128)(2,1)} %constant_dynamic-update-slice_fusion.12, f16[16,2,32,128]{3,2,1,0:T(8,128)(2,1)} %copy-done, f32[1,32,128]{2,1,0:T(8,128)S(1)} %get-tuple-element.25), kind=kLoop, calls=%fused_computation.19 | loop fusion | flops 45056 | bytes 73728
  79.1 1.4 %constant_dynamic-update-slice_fusion.9 = (f16[16,32,128]{2,1,0:T(8,128)(2,1)}, f32[1,32,128]{2,1,0:T(8,128)S(1)}) fusion(f16[16,32,128]{2,1,0:T(8,128)(2,1)} %constant_dynamic-update-slice_fusion.10, f16[16,2,32,128]{3,2,1,0:T(8,128)(2,1)} %copy-done, f32[1,32,128]{2,1,0:T(8,128)S(1)} %get-tuple-element.23), kind=kLoop, calls=%fused_computation.17 | loop fusion | flops 45056 | bytes 73728
  80.5 1.3 %constant_dynamic-update-slice_fusion.8 = f16[16,32,128]{2,1,0:T(8,128)(2,1)} fusion(f16[16,32,128]{2,1,0:T(8,128)(2,1)} %get-tuple-element.20, f16[16,2,32,128]{3,2,1,0:T(8,128)(2,1)} %copy-done, f32[1,32,128]{2,1,0:T(8,128)S(1)} %get-tuple-element.21), kind=kLoop, calls=%fused_computation.16 | loop fusion | flops 24576 | bytes 40960
  81.8 1.4 %constant_dynamic-update-slice_fusion.7 = (f16[16,32,128]{2,1,0:T(8,128)(2,1)}, f32[1,32,128]{2,1,0:T(8,128)S(1)}) fusion(f16[16,32,128]{2,1,0:T(8,128)(2,1)} %constant_dynamic-update-slice_fusion.8, f16[16,2,32,128]{3,2,1,0:T(8,128)(2,1)} %copy-done, f32[1,32,128]{2,1,0:T(8,128)S(1)} %get-tuple-element.21), kind=kLoop, calls=%fused_computation.15 | loop fusion | flops 45056 | bytes 73728
  84.5 1.4 %constant_dynamic-update-slice_fusion.5 = (f16[16,32,128]{2,1,0:T(8,128)(2,1)}, f32[1,32,128]{2,1,0:T(8,128)S(1)}) fusion(f16[16,32,128]{2,1,0:T(8,128)(2,1)} %constant_dynamic-update-slice_fusion.6, f16[16,2,32,128]{3,2,1,0:T(8,128)(2,1)} %copy-done, f32[1,32,128]{2,1,0:T(8,128)S(1)} %get-tuple-element.19), kind=kLoop, calls=%fused_computation.13 | loop fusion | flops 45056 | bytes 73728
  87.1 1.4 %constant_dynamic-update-slice_fusion.3 = (f16[16,32,128]{2,1,0:T(8,128)(2,1)}, f32[1,32,128]{2,1,0:T(8,128)S(1)}) fusion(f16[16,32,128]{2,1,0:T(8,128)(2,1)} %constant_dynamic-update-slice_fusion.4, f16[16,2,32,128]{3,2,1,0:T(8,128)(2,1)} %copy-done, f32[1,32,128]{2,1,0:T(8,128)S(1)} %get-tuple-element.17), kind=kLoop, calls=%fused_computation.11 | loop fusion | flops 45056 | bytes 73728
  89.8 1.4 %constant_dynamic-update-slice_fusion.1 = f16[16,32,128]{2,1,0:T(8,128)(2,1)} fusion(f16[16,32,128]{2,1,0:T(8,128)(2,1)} %constant_dynamic-update-slice_fusion.2, f16[16,2,32,128]{3,2,1,0:T(8,128)(2,1)} %copy-done, f32[1,32,128]{2,1,0:T(8,128)S(1)} %get-tuple-element.15), kind=kLoop, calls=%fused_computation.9 | loop fusion | flops 45056 | bytes 57344
  91.2 1.4 %constant_dynamic-update-slice_fusion = f16[16,32,128]{2,1,0:T(8,128)(2,1)} fusion(f16[16,32,128]{2,1,0:T(8,128)(2,1)} %constant_dynamic-update-slice_fusion.1, f16[16,2,32,128]{3,2,1,0:T(8,128)(2,1)} %copy-done, f32[1,32,128]{2,1,0:T(8,128)S(1)} %get-tuple-element.15), kind=kLoop, calls=%fused_computation.8 | loop fusion | flops 65536 | bytes 73728 | tf_op jit(solution)/shard_map/stack | solution.py:173
  92.6 6.0 %all-to-all-start.2 = ((f16[16,32,128]{2,1,0:T(8,128)(2,1)}), f16[16,32,128]{2,1,0:T(8,128)(2,1)S(1)}, u32[]{:S(2)}, u32[]{:S(2)}) async-start(f16[16,32,128]{2,1,0:T(8,128)(2,1)} %constant_dynamic-update-slice_fusion), calls=%async_computation.2 | async-start | bytes 262144 | tf_op jit(solution)/shard_map/all_to_all | solution.py:172
  99.8 13.4 %all-to-all-done.2 = f16[16,32,128]{2,1,0:T(8,128)(2,1)S(1)} async-done(((f16[16,32,128]{2,1,0:T(8,128)(2,1)}), f16[16,32,128]{2,1,0:T(8,128)(2,1)S(1)}, u32[]{:S(2)}, u32[]{:S(2)}) %all-to-all-start.2) | async-done | bytes 131104 | tf_op jit(solution)/shard_map/all_to_all | solution.py:172
  (40 shorter events, 15.2 us)
Async XLA Ops:
  0.6 12.6 %copy-start.4 = (bf16[9,64,32]{1,2,0:T(8,128)(2,1)S(1)}, bf16[9,64,32]{1,2,0:T(8,128)(2,1)}, u32[]{:S(2)}) copy-start(bf16[9,64,32]{1,2,0:T(8,128)(2,1)} %param.15) | copy-start | bytes 110596
  1.9 11.5 %copy-start.2 = (bf16[3,9,32,32]{3,2,1,0:T(8,128)(2,1)S(1)}, bf16[3,9,32,32]{3,2,1,0:T(8,128)(2,1)}, u32[]{:S(2)}) copy-start(bf16[3,9,32,32]{3,2,1,0:T(8,128)(2,1)} %param.13) | copy-start | bytes 165892
  1.9 18.5 %collective-permute-start = (bf16[16,32,128]{2,1,0:T(8,128)(2,1)S(1)}, bf16[16,32,128]{2,1,0:T(8,128)(2,1)S(1)}, u32[]{:S(2)}, u32[]{:S(2)}) collective-permute-start(bf16[16,32,128]{2,1,0:T(8,128)(2,1)S(1)} %fusion.3), channel_id=1, source_target_pairs={{0,8},{1,9},{2,10},{3,11},{4,12},{5,13},{6,14},{7,15},{8,16},{9,17... | collective-permute-start | bytes 393224 | tf_op jit(solution)/shard_map/ppermute | solution.py:127
  5.9 13.1 %collective-permute-start.2 = (bf16[4,32,128]{2,1,0:T(8,128)(2,1)S(1)}, bf16[4,32,128]{2,1,0:T(8,128)(2,1)S(1)}, u32[]{:S(2)}, u32[]{:S(2)}) collective-permute-start(bf16[4,32,128]{2,1,0:T(8,128)(2,1)S(1)} %get-tuple-element.28), channel_id=1, source_target_pairs={{1,8},{2,9},{3,10},{4,11},{5,12},{6,13},{7,14},{9,16},{10,17},{11,... | collective-permute-start | bytes 98312 | tf_op jit(solution)/shard_map/ppermute | solution.py:127
  8.7 11.7 %collective-permute-start.1 = (bf16[4,32,128]{2,1,0:T(8,128)(2,1)S(1)}, bf16[4,32,128]{2,1,0:T(8,128)(2,1)S(1)}, u32[]{:S(2)}, u32[]{:S(2)}) collective-permute-start(bf16[4,32,128]{2,1,0:T(8,128)(2,1)S(1)} %get-tuple-element.29), channel_id=1, source_target_pairs={{0,9},{1,10},{2,11},{3,12},{4,13},{5,14},{6,15},{8,17},{9,18},{10,... | collective-permute-start | bytes 98312 | tf_op jit(solution)/shard_map/ppermute | solution.py:127
  18.9 1.5 %copy-start.5 = (bf16[4,32,128]{2,1,0:T(8,128)(2,1)}, bf16[4,32,128]{2,1,0:T(8,128)(2,1)S(1)}, u32[]{:S(2)}) copy-start(bf16[4,32,128]{2,1,0:T(8,128)(2,1)S(1)} %collective-permute-done.2.high_ref) | copy-start | bytes 98308
  20.4 0.6 copy-start.6
  20.4 0.7 copy-start.3
  26.8 27.7 %all-to-all-start = ((f16[16,2,32,128]{3,2,1,0:T(8,128)(2,1)}), f16[16,2,32,128]{3,2,1,0:T(8,128)(2,1)S(1)}, u32[]{:S(2)}, u32[]{:S(2)}) async-start(f16[16,2,32,128]{3,2,1,0:T(8,128)(2,1)} %convert_element_type.1419), calls=%async_computation | async-start | bytes 524288 | tf_op jit(solution)/shard_map/all_to_all | solution.py:155
  54.6 0.8 copy-start
  55.4 10.3 %all-to-all-start.1 = ((f32[4,2,32,128]{3,2,1,0:T(8,128)}), f32[4,2,32,128]{3,2,1,0:T(8,128)S(1)}, u32[]{:S(2)}, u32[]{:S(2)}) async-start(f32[4,2,32,128]{3,2,1,0:T(8,128)} %broadcast_in_dim.29), calls=%async_computation.1 | async-start | bytes 262144 | tf_op jit(solution)/shard_map/all_to_all | solution.py:161
  65.6 0.7 copy-start.7
  66.9 25.7 %all-to-all-start.3 = ((f32[8,1,128]{2,1,0:T(1,128)}), f32[8,1,128]{2,1,0:T(1,128)S(1)}, u32[]{:S(2)}, u32[]{:S(2)}) async-start(f32[8,1,128]{2,1,0:T(1,128)} %broadcast_in_dim.32), calls=%async_computation.3 | async-start | bytes 8192 | tf_op jit(solution)/shard_map/all_to_all | solution.py:178
  75.1 38.1 %copy-start.1 = (f32[16,2,32,128]{3,2,1,0:T(8,128)S(1)}, f32[16,2,32,128]{3,2,1,0:T(8,128)}, u32[]{:S(2)}) copy-start(f32[16,2,32,128]{3,2,1,0:T(8,128)} %get-tuple-element.4) | copy-start | bytes 1572868
  92.6 20.7 %all-to-all-start.2 = ((f16[16,32,128]{2,1,0:T(8,128)(2,1)}), f16[16,32,128]{2,1,0:T(8,128)(2,1)S(1)}, u32[]{:S(2)}, u32[]{:S(2)}) async-start(f16[16,32,128]{2,1,0:T(8,128)(2,1)} %constant_dynamic-update-slice_fusion), calls=%async_computation.2 | async-start | bytes 262144 | tf_op jit(solution)/shard_map/all_to_all | solution.py:172

commit v2 on v1

v2 whole, which is shorter than its diff:
```python
import jax
import jax.numpy as jnp
from jax import lax
from jax.experimental import pallas as pl
from jax.experimental.pallas import tpu as pltpu
from jax.sharding import PartitionSpec as P


NX = 4
NZ = 16
HALO = 4
GROUP = 6
LIMIT = 16 * 2**20


def column(vec):
    n = vec.shape[1]
    rows = lax.broadcasted_iota(jnp.int32, (n, n), 0)
    cols = lax.broadcasted_iota(jnp.int32, (n, n), 1)
    return jnp.sum(jnp.where(rows == cols, jnp.broadcast_to(vec, (n, n)), 0.0), axis=1, keepdims=True)


def groups_of(rows):
    return [(g, min(GROUP, rows - g)) for g in range(0, rows, GROUP)]


def rounded(value):
    return value.astype(jnp.bfloat16).astype(jnp.float32)


def send_kernel(traj_ref, start_ref, act_ref, shift_ref, pair_ref, chip_ref, line_ref):
    chans, _ = shift_ref.shape[1:]
    rows = shift_ref.shape[0] - 1
    last = lax.axis_index("tm") == lax.axis_size("tm") - 1
    even = lax.rem(lax.axis_index("space"), 2) == 0
    line_ref[...] = jnp.zeros(line_ref.shape, jnp.float32)
    rest = act_ref[...]
    for part in range(3):
        piece = rounded(rest)
        line_ref[part : part + 1, : piece.shape[1]] = piece
        rest = rest - piece
    shift_ref[rows] = line_ref[...].astype(jnp.bfloat16)

    def guess(r):
        at = pl.ds(r, chans, stride=rows)
        return jnp.where(last, start_ref[at, :], traj_ref[at, :])

    for r in range(rows):
        shift_ref[r] = traj_ref[pl.ds(r, chans, stride=rows), :].astype(jnp.bfloat16)
    for r in range(HALO):
        upper, lower = guess(r), guess(rows - HALO + r)
        pair_ref[r] = jnp.where(even, lower, upper).astype(jnp.bfloat16)
        chip_ref[r] = jnp.where(even, upper, lower).astype(jnp.bfloat16)


def conv_kernel(
    shift_ref, pair_ref, chip_ref, traj_ref, start_ref, proj_ref, wh_ref, hb_ref, wo_ref, cb_ref, gb_ref, sk_ref,
    maps_ref, res_ref, xa_ref, xb_ref, band_ref, head_ref, guess_ref,
):
    strip = lax.axis_index("space")
    step_last = lax.axis_index("tm") == lax.axis_size("tm") - 1
    even = lax.rem(strip, 2) == 0
    chans, width = shift_ref.shape[1:]
    rows = shift_ref.shape[0] - 1
    lanes = lax.broadcasted_iota(jnp.int32, (chans, width), 1)
    first, last = lanes == 0, lanes == width - 1

    for ref in (xa_ref, xb_ref):
        ref[:, 3 * chans :, :] = jnp.zeros((ref.shape[0], ref.shape[1] - 3 * chans, width), jnp.bfloat16)
    band_ref[...] = jnp.zeros(band_ref.shape, jnp.bfloat16)
    head_ref[...] = jnp.zeros(head_ref.shape, jnp.bfloat16)

    parts = shift_ref[rows].astype(jnp.float32)
    line = parts[0:1] + parts[1:2] + parts[2:3]
    act = column(line[:, : proj_ref.shape[0]])
    terms = jnp.sum(act * proj_ref[...], axis=0, keepdims=True)
    biases = [column(hb_ref[l : l + 1, :]) for l in range(3)]
    biases[0] = biases[0] + column(terms[:, :chans])
    gate_bias = column(gb_ref[...]) + column(terms[:, chans:])
    cand_bias = column(cb_ref[...])
    skip = column(sk_ref[...])

    def put(ref, row, value):
        ref[row, :chans, :] = jnp.where(first, 0.0, pltpu.roll(value, 1, 1)).astype(jnp.bfloat16)
        ref[row, chans : 2 * chans, :] = value.astype(jnp.bfloat16)
        ref[row, 2 * chans : 3 * chans, :] = jnp.where(last, 0.0, pltpu.roll(value, width - 1, 1)).astype(jnp.bfloat16)

    for r in range(HALO):
        pair = pair_ref[r].astype(jnp.float32)
        chip = chip_ref[r].astype(jnp.float32)
        put(xa_ref, r, jnp.where(even, chip, pair))
        put(xa_ref, HALO + rows + r, jnp.where(even, pair, chip))
    for r in range(rows):
        at = pl.ds(r, chans, stride=rows)
        guess = jnp.where(step_last, start_ref[at, :], traj_ref[at, :])
        guess_ref[r] = guess
        put(xa_ref, HALO + r, guess)

    def product(band, outs, src, g, n):
        k = (n + 2) * 128
        rhs = src[g : g + n + 2].reshape(k, width)
        return jnp.dot(band[: n * outs, :k], rhs, preferred_element_type=jnp.float32)

    top = strip == 0
    bottom = strip == lax.axis_size("space") - 1
    src, dst = xa_ref, xb_ref
    for layer in range(3):
        for r in range(GROUP):
            for a in range(3):
                band_ref[r * chans : (r + 1) * chans, (r + a) * 128 : (r + a + 1) * 128] = wh_ref[layer, a]
        halo = HALO - 1 - layer
        for g, n in groups_of(rows + 2 * halo):
            acc = product(band_ref, chans, src, g, n).reshape(n, chans, width)
            for j in range(n):
                pre = acc[j] + biases[layer]
                value = 0.5 * pre * (1.0 + jnp.tanh(0.5 * pre))
                if g + j < halo:
                    value = jnp.where(top, 0.0, value)
                if g + j >= halo + rows:
                    value = jnp.where(bottom, 0.0, value)
                put(dst, g + j, value)
        src, dst = dst, src

    for r in range(GROUP):
        for a in range(3):
            head_ref[r * 2 * chans : (r + 1) * 2 * chans, (r + a) * 128 : (r + a + 1) * 128] = wo_ref[a]
    total = jnp.zeros((chans, width), jnp.float32)
    for g, n in groups_of(rows):
        acc = product(head_ref, 2 * chans, src, g, n).reshape(n, 2 * chans, width)
        for j in range(n):
            row = g + j
            guess = guess_ref[row]
            cand = jnp.tanh(acc[j, :chans] + cand_bias + skip * guess)
            rest = 1.0 / (1.0 + jnp.exp(acc[j, chans:] + gate_bias))
            slope = (1.0 - cand * cand) * skip
            maps_ref[row, 0] = rest * (1.0 - slope)
            maps_ref[row, 1] = rest * (cand - slope * guess)
            fval = guess + rest * (cand - guess)
            diff = shift_ref[row].astype(jnp.float32) - fval
            total = total + diff * diff
    res_ref[...] = jnp.sum(total, axis=0, keepdims=True)


def prefix_kernel(maps_ref, pref_ref):
    shape = maps_ref.shape[2:]
    pref_ref[0, 0] = jnp.ones(shape, jnp.float32)
    pref_ref[0, 1] = jnp.zeros(shape, jnp.float32)
    a = 1.0 - maps_ref[0, 0]
    b = maps_ref[0, 1]
    for z in range(1, maps_ref.shape[0]):
        pref_ref[z, 0] = a
        pref_ref[z, 1] = b
        keep = 1.0 - maps_ref[z, 0]
        a, b = keep * a, keep * b + maps_ref[z, 1]


def tap_rows(weights, outs):
    lead = weights.shape[:-3]
    chans = weights.shape[-1]
    split = weights.reshape(lead + (3, 3, outs, chans))
    moved = jnp.swapaxes(split, -3, -2).reshape(lead + (3, outs, 3 * chans))
    return jnp.pad(moved, [(0, 0)] * (len(lead) + 2) + [(0, 128 - 3 * chans)])


def params():
    return pltpu.CompilerParams(vmem_limit_bytes=LIMIT)


def body(traj, start_state, actions, hidden_w, hidden_b, head_w, cand_b, gate_b, skip, act_proj):
    _, chans, rows, width = traj.shape
    n_tm, n_space = lax.axis_size("tm"), lax.axis_size("space")
    place = lax.axis_index("tm")
    mine = place // NZ
    f32, bf16 = jnp.float32, jnp.bfloat16
    flat = traj.reshape(chans * rows, width)
    begin = start_state.reshape(chans * rows, width)

    shift, pair, chip = pl.pallas_call(
        send_kernel,
        out_shape=(
            jax.ShapeDtypeStruct((rows + 1, chans, width), bf16),
            jax.ShapeDtypeStruct((HALO, chans, width), bf16),
            jax.ShapeDtypeStruct((HALO, chans, width), bf16),
        ),
        scratch_shapes=[pltpu.VMEM((chans, width), f32)],
        compiler_params=params(),
        name="sends",
    )(flat, begin, actions)
    shift = lax.ppermute(shift, "tm", [((t + 1) % n_tm, t) for t in range(n_tm)])
    pair = lax.ppermute(pair, "space", [(s, s ^ 1) for s in range(n_space)])
    crossing = [(s, s + 1) for s in range(1, n_space - 1, 2)]
    chip = lax.ppermute(chip, "space", crossing + [(b, a) for a, b in crossing])

    kb = (GROUP + 2) * 128
    maps, partial = pl.pallas_call(
        conv_kernel,
        out_shape=(
            jax.ShapeDtypeStruct((rows, 2, chans, width), f32),
            jax.ShapeDtypeStruct((1, width), f32),
        ),
        scratch_shapes=[
            pltpu.VMEM((rows + 2 * HALO, 128, width), bf16),
            pltpu.VMEM((rows + 2 * HALO, 128, width), bf16),
            pltpu.VMEM((GROUP * chans, kb), bf16),
            pltpu.VMEM((GROUP * 2 * chans, kb), bf16),
            pltpu.VMEM((rows, chans, width), f32),
        ],
        compiler_params=params(),
        name="dynamics",
    )(
        shift, pair, chip, flat, begin, act_proj,
        tap_rows(hidden_w, chans), hidden_b, tap_rows(head_w, 2 * chans),
        cand_b[None], gate_b[None], skip[None],
    )

    z_groups = [[x * NZ + z for z in range(NZ)] for x in range(NX)]
    x_groups = [[x * NZ + z for x in range(NX)] for z in range(NZ)]
    sent = lax.all_to_all(maps.astype(jnp.float16), "tm", 0, 0, axis_index_groups=z_groups)
    for bit in (1, 2):
        partial = partial + lax.ppermute(partial, "space", [(s, s ^ bit) for s in range(n_space)])
    sent, partial = lax.optimization_barrier((sent, partial))

    steps = [(1.0 - sent[z, 0].astype(f32), sent[z, 1].astype(f32)) for z in range(NZ)]
    block_a, block_b = steps[0]
    for a, b in steps[1:]:
        block_a, block_b = a * block_a, a * block_b + b
    final = mine == NX - 1
    block = jnp.stack([jnp.where(final, steps[-1][0], block_a), jnp.where(final, steps[-1][1], block_b)])
    blocks = lax.all_to_all(
        jnp.broadcast_to(block[None], (NX,) + block.shape), "tm", 0, 0, axis_index_groups=x_groups
    )
    pref = pl.pallas_call(
        prefix_kernel,
        out_shape=jax.ShapeDtypeStruct((NZ, 2, chans, width), f32),
        compiler_params=params(),
        cost_estimate=pl.CostEstimate(flops=2**20, bytes_accessed=2**20, transcendentals=0),
        name="prefix",
    )(sent.astype(f32))
    state = lax.dynamic_index_in_dim(start_state, place % NZ, 1, False)
    state = blocks[NX - 1, 0] * state + blocks[NX - 1, 1]
    for x in range(NX - 1):
        state = jnp.where(x < mine, blocks[x, 0] * state + blocks[x, 1], state)
    states = (pref[:, 0] * state + pref[:, 1]).astype(jnp.float16)
    back = lax.all_to_all(states, "tm", 0, 0, axis_index_groups=z_groups)
    partial = partial + lax.ppermute(partial, "space", [(s, s ^ 4) for s in range(n_space)])
    res_msq = jnp.sum(partial).reshape(1) / (chans * rows * width * n_space)
    res_msq = lax.ppermute(res_msq, "tm", [(t, (t + 1) % n_tm) for t in range(n_tm)])
    back, res_msq = lax.optimization_barrier((back, res_msq))
    new_traj = jnp.swapaxes(back.astype(f32), 0, 1)[None]
    return new_traj, res_msq


def solution(mesh):
    return jax.shard_map(
        body,
        mesh=mesh,
        in_specs=(
            P("tm", None, "space", None),
            P(None, "space", None),
            P("tm", None),
            P(),
            P(),
            P(),
            P(),
            P(),
            P(),
            P(),
        ),
        out_specs=(P("tm", None, "space", None), P("tm")),
        check_vma=False,
    )
```

time: 117 us -> 88.8 us (0.76)
  other arithmetic: 24.5 us -> 2.26 us
  waiting for transfers between devices: 42.4 us -> 31.3 us
  starting transfers between devices: 35.7 us -> 43.7 us
  Pallas kernels: 3.99 us -> 2.31 us
    unnamed x15 -> x0, other arithmetic: 19.4 us -> none
    ppermute x3 -> x7, starting transfers between devices: 11.3 us -> 29.4 us  [the longest x1 13.6 us: body(): lax.ppermute(shift, 'tm', [((t + 1) % n_tm, t) for t in range(n_tm)])]
    all_to_all x2 -> x1, waiting for transfers between devices: 13.4 us -> 0.01 us  [body(): back = lax.all_to_all(states, 'tm', 0, 0, axis_index_groups=z_groups)]
    ppermute x3 -> x7, waiting for transfers between devices: 5.42 us -> 15.1 us  [the longest x1 5.04 us: body(): lax.ppermute(partial, 'space', [(s, s ^ 4) for s in range(n_space)])]
    all_to_all x1, waiting for transfers between devices: 18.5 us -> 10.3 us  [body(): lax.all_to_all(maps.astype(jnp.float16), 'tm', 0, 0, axis_index_groups=z_...]
    all_to_all x1, starting transfers between devices: 9.19 us -> 4.07 us  [body(): lax.all_to_all(maps.astype(jnp.float16), 'tm', 0, 0, axis_index_groups=z_...]
    all_to_all x2 -> x1, starting transfers between devices: 10.9 us -> 5.98 us  [body(): back = lax.all_to_all(states, 'tm', 0, 0, axis_index_groups=z_groups)]
    unnamed x17 -> x25, local copies, waits for them, and re-layouts: 2.19 us -> 4.09 us
  transfers between devices with their start and end apart: 7 -> 10, of which waited for: 5 -> 7; matrix products, arithmetic and copies ran while one was open for 21% -> 1% of each run, Pallas kernels for 0% -> 0%
where the time goes in v2:
time: 88.8 us; the launch traced here: 88.1 us
  starting transfers between devices  43.7 us (49%)
  waiting for transfers between devices  31.3 us (35%)
  local copies, waits for them, and re-layouts  5.22 us (6%)
  between operations  3.35 us (4%)
  Pallas kernels  2.31 us (3%)
  other arithmetic  2.26 us (3%)
    ppermute x1, starting transfers between devices, body(): lax.ppermute(shift, 'tm', [((t + 1) % n_tm, t) for t in range(n_tm)])  13.6 us
    all_to_all x1, waiting for transfers between devices, body(): lax.all_to_all(maps.astype(jnp.float16), 'tm', 0, 0, axis_index_groups=z_...  10.3 us
    all_to_all x1, starting transfers between devices, body(): back = lax.all_to_all(states, 'tm', 0, 0, axis_index_groups=z_groups)  5.98 us
    all_to_all x1, waiting for transfers between devices, body(): lax.all_to_all(jnp.broadcast_to(block[None], (NX,) + block.shape), 'tm',...  5.85 us
    ppermute x1, starting transfers between devices, body(): lax.ppermute(res_msq, 'tm', [(t, (t + 1) % n_tm) for t in range(n_tm)])  5.1 us
    ppermute x1, waiting for transfers between devices, body(): lax.ppermute(partial, 'space', [(s, s ^ 4) for s in range(n_space)])  5.04 us
    ppermute x2, starting transfers between devices, body(): lax.ppermute(partial, 'space', [(s, s ^ bit) for s in range(n_space)])  4.35 us
    all_to_all x1, starting transfers between devices, body(): lax.all_to_all(jnp.broadcast_to(block[None], (NX,) + block.shape), 'tm',...  4.28 us
  transfers between devices with their start and end apart: 10, of which 7 were waited for; matrix products, arithmetic and copies ran while one was open for 1% of the time, Pallas kernels for 0%

profile of v2, /device:TPU:8, one launch (start us, length us, event | category | flops | bytes accessed | tf_op | source)
XLA Modules:
  0.0 88.1 jit_solution(4674077502730648345)
XLA Ops:
  1.3 0.9 %copy-done = f32[32,16,128]{2,1,0:T(8,128)S(1)} copy-done((f32[32,16,128]{2,1,0:T(8,128)S(1)}, f32[32,16,128]{2,1,0:T(8,128)}, u32[]{:S(2)}) %copy-start) | copy-done | bytes 262168
  2.2 0.9 %copy-done.2 = f32[1,32,16,128]{3,2,1,0:T(8,128)S(1)} copy-done((f32[1,32,16,128]{3,2,1,0:T(8,128)S(1)}, f32[1,32,16,128]{3,2,1,0:T(8,128)}, u32[]{:S(2)}) %copy-start.2) | copy-done | bytes 262168
  3.3 13.6 %collective-permute-start = (bf16[17,32,128]{2,1,0:T(8,128)(2,1)S(1)}, bf16[17,32,128]{2,1,0:T(8,128)(2,1)S(1)}, u32[]{:S(2)}, u32[]{:S(2)}) collective-permute-start(bf16[17,32,128]{2,1,0:T(8,128)(2,1)S(1)} %get-tuple-element.11), channel_id=1, source_target_pairs={{8,0},{16,8},{24,16},{32,24},{40,32},{48,40},{56,48},{64,56},{72,6... | collective-permute-start | bytes 417800 | tf_op jit(solution)/shard_map/ppermute | solution.py:189
  16.9 1.9 %collective-permute-start.1 = (bf16[4,32,128]{2,1,0:T(8,128)(2,1)S(1)}, bf16[4,32,128]{2,1,0:T(8,128)(2,1)S(1)}, u32[]{:S(2)}, u32[]{:S(2)}) collective-permute-start(bf16[4,32,128]{2,1,0:T(8,128)(2,1)S(1)} %get-tuple-element.12), channel_id=1, source_target_pairs={{0,1},{1,0},{2,3},{3,2},{4,5},{5,4},{6,7},{7,6},{8,9},{9,8},{10,11... | collective-permute-start | bytes 98312 | tf_op jit(solution)/shard_map/ppermute | solution.py:190
  18.9 2.5 %collective-permute-start.2 = (bf16[4,32,128]{2,1,0:T(8,128)(2,1)S(1)}, bf16[4,32,128]{2,1,0:T(8,128)(2,1)S(1)}, u32[]{:S(2)}, u32[]{:S(2)}) collective-permute-start(bf16[4,32,128]{2,1,0:T(8,128)(2,1)S(1)} %get-tuple-element.13), channel_id=1, source_target_pairs={{1,2},{3,4},{5,6},{2,1},{4,3},{6,5},{9,10},{11,12},{13,14},{10,9},... | collective-permute-start | bytes 98312 | tf_op jit(solution)/shard_map/ppermute | solution.py:192
  21.9 2.2 %collective-permute-done.2.chip_ref = bf16[4,32,128]{2,1,0:T(8,128)(2,1)S(1)} collective-permute-done((bf16[4,32,128]{2,1,0:T(8,128)(2,1)S(1)}, bf16[4,32,128]{2,1,0:T(8,128)(2,1)S(1)}, u32[]{:S(2)}, u32[]{:S(2)}) %collective-permute-start.2) | collective-permute-done | bytes 32800 | tf_op jit(solution)/shard_map/ppermute | solution.py:192
  24.8 2.1 %dynamics.1 = (f32[16,2,32,128]{3,2,1,0:T(8,128)S(1)}, f32[1,128]{1,0:T(1,128)S(1)}) custom-call(bf16[17,32,128]{2,1,0:T(8,128)(2,1)S(1)} %collective-permute-done.shift_ref, bf16[4,32,128]{2,1,0:T(8,128)(2,1)S(1)} %collective-permute-done.1.pair_ref, bf16[4,32,128]{2,1,0:T(8,128)(2,1)S(1)} %collective-permute-done.2.chip_ref, f32[512,128]{1,0:T(8,128)S(1)} %bitcast.175, ...), custom_call_target="tpu_custom_call" | custom-call | tf_op jit(solution)/shard_map/dynamics/pallas_call | solution.py:195
  26.9 0.8 convert_element_type.454
  27.7 4.1 %all-to-all-start = ((f16[16,2,32,128]{3,2,1,0:T(8,128)(2,1)}), f16[16,2,32,128]{3,2,1,0:T(8,128)(2,1)S(1)}, u32[]{:S(2)}, u32[]{:S(2)}) async-start(f16[16,2,32,128]{3,2,1,0:T(8,128)(2,1)} %convert_element_type.454), calls=%async_computation | async-start | bytes 524288 | tf_op jit(solution)/shard_map/all_to_all | solution.py:218
  31.8 2.1 %collective-permute-start.3 = (f32[1,128]{1,0:T(1,128)S(1)}, f32[1,128]{1,0:T(1,128)S(1)}, u32[]{:S(2)}, u32[]{:S(2)}) collective-permute-start(f32[1,128]{1,0:T(1,128)S(1)} %get-tuple-element.15), channel_id=1, source_target_pairs={{0,1},{1,0},{2,3},{3,2},{4,5},{5,4},{6,7},{7,6},{8,9},{9,8},{10,11... | collective-permute-start | bytes 1544 | tf_op jit(solution)/shard_map/ppermute | solution.py:220
  33.9 0.9 %collective-permute-done.3 = f32[1,128]{1,0:T(1,128)S(1)} collective-permute-done((f32[1,128]{1,0:T(1,128)S(1)}, f32[1,128]{1,0:T(1,128)S(1)}, u32[]{:S(2)}, u32[]{:S(2)}) %collective-permute-start.3) | collective-permute-done | bytes 544 | tf_op jit(solution)/shard_map/ppermute | solution.py:220
  34.9 2.2 %collective-permute-start.4 = (f32[1,128]{1,0:T(1,128)S(1)}, f32[1,128]{1,0:T(1,128)S(1)}, u32[]{:S(2)}, u32[]{:S(2)}) collective-permute-start(f32[1,128]{1,0:T(1,128)S(1)} %add.206), channel_id=1, source_target_pairs={{0,2},{1,3},{2,0},{3,1},{4,6},{5,7},{6,4},{7,5},{8,10},{9,11},{10,... | collective-permute-start | bytes 1544 | tf_op jit(solution)/shard_map/ppermute | solution.py:220
  37.1 3.2 %collective-permute-done.4 = f32[1,128]{1,0:T(1,128)S(1)} collective-permute-done((f32[1,128]{1,0:T(1,128)S(1)}, f32[1,128]{1,0:T(1,128)S(1)}, u32[]{:S(2)}, u32[]{:S(2)}) %collective-permute-start.4) | collective-permute-done | bytes 544 | tf_op jit(solution)/shard_map/ppermute | solution.py:220
  40.3 10.3 %all-to-all-done = f16[16,2,32,128]{3,2,1,0:T(8,128)(2,1)S(1)} async-done(((f16[16,2,32,128]{3,2,1,0:T(8,128)(2,1)}), f16[16,2,32,128]{3,2,1,0:T(8,128)(2,1)S(1)}, u32[]{:S(2)}, u32[]{:S(2)}) %all-to-all-start) | async-done | bytes 262176 | tf_op jit(solution)/shard_map/all_to_all | solution.py:218
  50.7 0.7 broadcast_in_dim.25
  51.4 4.3 %all-to-all-start.1 = ((f32[4,2,32,128]{3,2,1,0:T(8,128)}), f32[4,2,32,128]{3,2,1,0:T(8,128)S(1)}, u32[]{:S(2)}, u32[]{:S(2)}) async-start(f32[4,2,32,128]{3,2,1,0:T(8,128)} %broadcast_in_dim.25), calls=%async_computation.1 | async-start | bytes 262144 | tf_op jit(solution)/shard_map/all_to_all | solution.py:229
  55.8 5.9 %all-to-all-done.1 = f32[4,2,32,128]{3,2,1,0:T(8,128)S(1)} async-done(((f32[4,2,32,128]{3,2,1,0:T(8,128)}), f32[4,2,32,128]{3,2,1,0:T(8,128)S(1)}, u32[]{:S(2)}, u32[]{:S(2)}) %all-to-all-start.1) | async-done | bytes 131104 | tf_op jit(solution)/shard_map/all_to_all | solution.py:229
  61.7 0.7 fusion.1
  62.4 6.0 %all-to-all-start.2 = ((f16[16,32,128]{2,1,0:T(8,128)(2,1)}), f16[16,32,128]{2,1,0:T(8,128)(2,1)S(1)}, u32[]{:S(2)}, u32[]{:S(2)}) async-start(f16[16,32,128]{2,1,0:T(8,128)(2,1)} %fusion.1), calls=%async_computation.2 | async-start | bytes 262144 | tf_op jit(solution)/shard_map/all_to_all | solution.py:244
  68.4 1.9 %collective-permute-start.5 = (f32[1,128]{1,0:T(1,128)S(1)}, f32[1,128]{1,0:T(1,128)S(1)}, u32[]{:S(2)}, u32[]{:S(2)}) collective-permute-start(f32[1,128]{1,0:T(1,128)S(1)} %add.207), channel_id=1, source_target_pairs={{0,4},{1,5},{2,6},{3,7},{4,0},{5,1},{6,2},{7,3},{8,12},{9,13},{10,... | collective-permute-start | bytes 1544 | tf_op jit(solution)/shard_map/ppermute | solution.py:245
  70.3 5.0 %collective-permute-done.5 = f32[1,128]{1,0:T(1,128)S(1)} collective-permute-done((f32[1,128]{1,0:T(1,128)S(1)}, f32[1,128]{1,0:T(1,128)S(1)}, u32[]{:S(2)}, u32[]{:S(2)}) %collective-permute-start.5) | collective-permute-done | bytes 544 | tf_op jit(solution)/shard_map/ppermute | solution.py:245
  76.6 5.1 %collective-permute-start.6 = (f32[1]{0:T(128)}, f32[1]{0:T(128)}, u32[]{:S(2)}, u32[]{:S(2)}) collective-permute-start(f32[1]{0:T(128)} %bitcast.40), channel_id=1, source_target_pairs={{0,8},{8,16},{16,24},{24,32},{32,40},{40,48},{48,56},{56,64},{64,7... | collective-permute-start | bytes 20 | tf_op jit(solution)/shard_map/ppermute | solution.py:247
  81.7 3.8 %collective-permute-done.6 = f32[1]{0:T(128)} collective-permute-done((f32[1]{0:T(128)}, f32[1]{0:T(128)}, u32[]{:S(2)}, u32[]{:S(2)}) %collective-permute-start.6) | collective-permute-done | bytes 36 | tf_op jit(solution)/shard_map/ppermute | solution.py:247
  85.5 0.9 copy.19
  (42 shorter events, 2.8 us)
Async XLA Ops:
  0.6 0.7 copy-start.6
  1.3 0.9 %copy-start = (f32[32,16,128]{2,1,0:T(8,128)S(1)}, f32[32,16,128]{2,1,0:T(8,128)}, u32[]{:S(2)}) copy-start(f32[32,16,128]{2,1,0:T(8,128)} %param.11) | copy-start | bytes 786436
  2.2 0.9 %copy-start.2 = (f32[1,32,16,128]{3,2,1,0:T(8,128)S(1)}, f32[1,32,16,128]{3,2,1,0:T(8,128)}, u32[]{:S(2)}) copy-start(f32[1,32,16,128]{3,2,1,0:T(8,128)} %param.10) | copy-start | bytes 786436
  3.2 18.2 %copy-start.11 = (bf16[9,64,32]{1,2,0:T(8,128)(2,1)S(1)}, bf16[9,64,32]{1,2,0:T(8,128)(2,1)}, u32[]{:S(2)}) copy-start(bf16[9,64,32]{1,2,0:T(8,128)(2,1)} %param.15) | copy-start | bytes 110596
  3.2 18.3 %copy-start.10 = (bf16[3,9,32,32]{3,2,1,0:T(8,128)(2,1)S(1)}, bf16[3,9,32,32]{3,2,1,0:T(8,128)(2,1)}, u32[]{:S(2)}) copy-start(bf16[3,9,32,32]{3,2,1,0:T(8,128)(2,1)} %param.13) | copy-start | bytes 165892
  3.3 20.8 %collective-permute-start = (bf16[17,32,128]{2,1,0:T(8,128)(2,1)S(1)}, bf16[17,32,128]{2,1,0:T(8,128)(2,1)S(1)}, u32[]{:S(2)}, u32[]{:S(2)}) collective-permute-start(bf16[17,32,128]{2,1,0:T(8,128)(2,1)S(1)} %get-tuple-element.11), channel_id=1, source_target_pairs={{8,0},{16,8},{24,16},{32,24},{40,32},{48,40},{56,48},{64,56},{72,6... | collective-permute-start | bytes 417800 | tf_op jit(solution)/shard_map/ppermute | solution.py:189
  16.9 4.9 %collective-permute-start.1 = (bf16[4,32,128]{2,1,0:T(8,128)(2,1)S(1)}, bf16[4,32,128]{2,1,0:T(8,128)(2,1)S(1)}, u32[]{:S(2)}, u32[]{:S(2)}) collective-permute-start(bf16[4,32,128]{2,1,0:T(8,128)(2,1)S(1)} %get-tuple-element.12), channel_id=1, source_target_pairs={{0,1},{1,0},{2,3},{3,2},{4,5},{5,4},{6,7},{7,6},{8,9},{9,8},{10,11... | collective-permute-start | bytes 98312 | tf_op jit(solution)/shard_map/ppermute | solution.py:190
  18.9 5.2 %collective-permute-start.2 = (bf16[4,32,128]{2,1,0:T(8,128)(2,1)S(1)}, bf16[4,32,128]{2,1,0:T(8,128)(2,1)S(1)}, u32[]{:S(2)}, u32[]{:S(2)}) collective-permute-start(bf16[4,32,128]{2,1,0:T(8,128)(2,1)S(1)} %get-tuple-element.13), channel_id=1, source_target_pairs={{1,2},{3,4},{5,6},{2,1},{4,3},{6,5},{9,10},{11,12},{13,14},{10,9},... | collective-permute-start | bytes 98312 | tf_op jit(solution)/shard_map/ppermute | solution.py:192
  21.6 2.5 %copy-start.1 = (f32[32,16,128]{2,1,0:T(8,128)S(1)}, f32[32,16,128]{2,1,0:T(8,128)}, u32[]{:S(2)}) copy-start(f32[32,16,128]{2,1,0:T(8,128)} %param.11) | copy-start | bytes 786436
  21.6 2.5 %copy-start.3 = (f32[1,32,16,128]{3,2,1,0:T(8,128)S(1)}, f32[1,32,16,128]{3,2,1,0:T(8,128)}, u32[]{:S(2)}) copy-start(f32[1,32,16,128]{3,2,1,0:T(8,128)} %param.10) | copy-start | bytes 786436
  21.8 2.3 %copy-start.4 = (f32[16,64]{1,0:T(8,128)S(1)}, f32[16,64]{1,0:T(8,128)}, u32[]{:S(2)}) copy-start(f32[16,64]{1,0:T(8,128)} %proj_ref.1) | copy-start | bytes 12292
  24.1 0.7 copy-start.5
  24.1 0.7 copy-start.7
  24.1 0.7 copy-start.8
  24.1 0.7 copy-start.9
  27.7 22.9 %all-to-all-start = ((f16[16,2,32,128]{3,2,1,0:T(8,128)(2,1)}), f16[16,2,32,128]{3,2,1,0:T(8,128)(2,1)S(1)}, u32[]{:S(2)}, u32[]{:S(2)}) async-start(f16[16,2,32,128]{3,2,1,0:T(8,128)(2,1)} %convert_element_type.454), calls=%async_computation | async-start | bytes 524288 | tf_op jit(solution)/shard_map/all_to_all | solution.py:218
  31.8 3.1 %collective-permute-start.3 = (f32[1,128]{1,0:T(1,128)S(1)}, f32[1,128]{1,0:T(1,128)S(1)}, u32[]{:S(2)}, u32[]{:S(2)}) collective-permute-start(f32[1,128]{1,0:T(1,128)S(1)} %get-tuple-element.15), channel_id=1, source_target_pairs={{0,1},{1,0},{2,3},{3,2},{4,5},{5,4},{6,7},{7,6},{8,9},{9,8},{10,11... | collective-permute-start | bytes 1544 | tf_op jit(solution)/shard_map/ppermute | solution.py:220
  34.9 5.5 %collective-permute-start.4 = (f32[1,128]{1,0:T(1,128)S(1)}, f32[1,128]{1,0:T(1,128)S(1)}, u32[]{:S(2)}, u32[]{:S(2)}) collective-permute-start(f32[1,128]{1,0:T(1,128)S(1)} %add.206), channel_id=1, source_target_pairs={{0,2},{1,3},{2,0},{3,1},{4,6},{5,7},{6,4},{7,5},{8,10},{9,11},{10,... | collective-permute-start | bytes 1544 | tf_op jit(solution)/shard_map/ppermute | solution.py:220
  51.4 10.3 %all-to-all-start.1 = ((f32[4,2,32,128]{3,2,1,0:T(8,128)}), f32[4,2,32,128]{3,2,1,0:T(8,128)S(1)}, u32[]{:S(2)}, u32[]{:S(2)}) async-start(f32[4,2,32,128]{3,2,1,0:T(8,128)} %broadcast_in_dim.25), calls=%async_computation.1 | async-start | bytes 262144 | tf_op jit(solution)/shard_map/all_to_all | solution.py:229
  62.4 23.1 %all-to-all-start.2 = ((f16[16,32,128]{2,1,0:T(8,128)(2,1)}), f16[16,32,128]{2,1,0:T(8,128)(2,1)S(1)}, u32[]{:S(2)}, u32[]{:S(2)}) async-start(f16[16,32,128]{2,1,0:T(8,128)(2,1)} %fusion.1), calls=%async_computation.2 | async-start | bytes 262144 | tf_op jit(solution)/shard_map/all_to_all | solution.py:244
  68.4 7.0 %collective-permute-start.5 = (f32[1,128]{1,0:T(1,128)S(1)}, f32[1,128]{1,0:T(1,128)S(1)}, u32[]{:S(2)}, u32[]{:S(2)}) collective-permute-start(f32[1,128]{1,0:T(1,128)S(1)} %add.207), channel_id=1, source_target_pairs={{0,4},{1,5},{2,6},{3,7},{4,0},{5,1},{6,2},{7,3},{8,12},{9,13},{10,... | collective-permute-start | bytes 1544 | tf_op jit(solution)/shard_map/ppermute | solution.py:245
  76.6 8.9 %collective-permute-start.6 = (f32[1]{0:T(128)}, f32[1]{0:T(128)}, u32[]{:S(2)}, u32[]{:S(2)}) collective-permute-start(f32[1]{0:T(128)} %bitcast.40), channel_id=1, source_target_pairs={{0,8},{8,16},{16,24},{24,32},{32,40},{40,48},{48,56},{56,64},{64,7... | collective-permute-start | bytes 20 | tf_op jit(solution)/shard_map/ppermute | solution.py:247

commit v3 on v2

--- a/solution.py
+++ b/solution.py
@@ -28,9 +28,29 @@
     return value.astype(jnp.bfloat16).astype(jnp.float32)
 
 
-def send_kernel(traj_ref, start_ref, act_ref, shift_ref, pair_ref, chip_ref, line_ref):
-    chans, _ = shift_ref.shape[1:]
-    rows = shift_ref.shape[0] - 1
+def send_kernel(
+    traj_hbm, start_hbm, hb_hbm, cb_hbm, gb_hbm, sk_hbm, proj_hbm, act_ref,
+    own_ref, pair_ref, chip_ref, guess_ref, cols_ref, line_ref, proj_ref,
+    traj_ref, start_ref, hb_ref, cb_ref, gb_ref, sk_ref, sems,
+):
+    chans, width = own_ref.shape[1:]
+    rows = own_ref.shape[0]
+    moves = [
+        pltpu.make_async_copy(source, target, sems.at[i])
+        for i, (source, target) in enumerate(
+            (
+                (traj_hbm, traj_ref),
+                (start_hbm, start_ref),
+                (hb_hbm, hb_ref),
+                (cb_hbm, cb_ref),
+                (gb_hbm, gb_ref),
+                (sk_hbm, sk_ref),
+                (proj_hbm, proj_ref),
+            )
+        )
+    ]
+    for move in moves:
+        move.start()
     last = lax.axis_index("tm") == lax.axis_size("tm") - 1
     even = lax.rem(lax.axis_index("space"), 2) == 0
     line_ref[...] = jnp.zeros(line_ref.shape, jnp.float32)
@@ -39,29 +59,36 @@
         piece = rounded(rest)
         line_ref[part : part + 1, : piece.shape[1]] = piece
         rest = rest - piece
-    shift_ref[rows] = line_ref[...].astype(jnp.bfloat16)
-
-    def guess(r):
+    pair_ref[HALO] = line_ref[...].astype(jnp.bfloat16)
+    for move in moves:
+        move.wait()
+
+    def spread(vec):
+        return jnp.broadcast_to(column(vec), (chans, width))
+
+    for i in range(3):
+        cols_ref[i] = spread(hb_ref[i : i + 1, :])
+    cols_ref[3] = spread(cb_ref[...])
+    cols_ref[4] = spread(gb_ref[...])
+    cols_ref[5] = spread(sk_ref[...])
+    for r in range(rows):
         at = pl.ds(r, chans, stride=rows)
-        return jnp.where(last, start_ref[at, :], traj_ref[at, :])
-
-    for r in range(rows):
-        shift_ref[r] = traj_ref[pl.ds(r, chans, stride=rows), :].astype(jnp.bfloat16)
+        mine = traj_ref[at, :]
+        own_ref[r] = mine.astype(jnp.bfloat16)
+        guess_ref[r] = jnp.where(last, start_ref[at, :], mine)
     for r in range(HALO):
-        upper, lower = guess(r), guess(rows - HALO + r)
+        upper, lower = guess_ref[r], guess_ref[rows - HALO + r]
         pair_ref[r] = jnp.where(even, lower, upper).astype(jnp.bfloat16)
         chip_ref[r] = jnp.where(even, upper, lower).astype(jnp.bfloat16)
 
 
 def conv_kernel(
-    shift_ref, pair_ref, chip_ref, traj_ref, start_ref, proj_ref, wh_ref, hb_ref, wo_ref, cb_ref, gb_ref, sk_ref,
-    maps_ref, res_ref, xa_ref, xb_ref, band_ref, head_ref, guess_ref,
+    guess_ref, pair_ref, chip_ref, line_ref, proj_ref, cols_ref, wh_ref, wo_ref,
+    maps_ref, xa_ref, xb_ref, band_ref, head_ref,
 ):
     strip = lax.axis_index("space")
-    step_last = lax.axis_index("tm") == lax.axis_size("tm") - 1
     even = lax.rem(strip, 2) == 0
-    chans, width = shift_ref.shape[1:]
-    rows = shift_ref.shape[0] - 1
+    rows, chans, width = guess_ref.shape
     lanes = lax.broadcasted_iota(jnp.int32, (chans, width), 1)
     first, last = lanes == 0, lanes == width - 1
 
@@ -70,15 +97,14 @@
     band_ref[...] = jnp.zeros(band_ref.shape, jnp.bfloat16)
     head_ref[...] = jnp.zeros(head_ref.shape, jnp.bfloat16)
 
-    parts = shift_ref[rows].astype(jnp.float32)
+    parts = jnp.where(even, line_ref[...], pair_ref[HALO].astype(jnp.float32))
     line = parts[0:1] + parts[1:2] + parts[2:3]
     act = column(line[:, : proj_ref.shape[0]])
     terms = jnp.sum(act * proj_ref[...], axis=0, keepdims=True)
-    biases = [column(hb_ref[l : l + 1, :]) for l in range(3)]
-    biases[0] = biases[0] + column(terms[:, :chans])
-    gate_bias = column(gb_ref[...]) + column(terms[:, chans:])
-    cand_bias = column(cb_ref[...])
-    skip = column(sk_ref[...])
+    biases = [cols_ref[0] + column(terms[:, :chans]), cols_ref[1], cols_ref[2]]
+    cand_bias = cols_ref[3]
+    gate_bias = cols_ref[4] + column(terms[:, chans:])
+    skip = cols_ref[5]
 
     def put(ref, row, value):
         ref[row, :chans, :] = jnp.where(first, 0.0, pltpu.roll(value, 1, 1)).astype(jnp.bfloat16)
@@ -91,10 +117,7 @@
         put(xa_ref, r, jnp.where(even, chip, pair))
         put(xa_ref, HALO + rows + r, jnp.where(even, pair, chip))
     for r in range(rows):
-        at = pl.ds(r, chans, stride=rows)
-        guess = jnp.where(step_last, start_ref[at, :], traj_ref[at, :])
-        guess_ref[r] = guess
-        put(xa_ref, HALO + r, guess)
+        put(xa_ref, HALO + r, guess_ref[r])
 
     def product(band, outs, src, g, n):
         k = (n + 2) * 128
@@ -124,7 +147,6 @@
     for r in range(GROUP):
         for a in range(3):
             head_ref[r * 2 * chans : (r + 1) * 2 * chans, (r + a) * 128 : (r + a + 1) * 128] = wo_ref[a]
-    total = jnp.zeros((chans, width), jnp.float32)
     for g, n in groups_of(rows):
         acc = product(head_ref, 2 * chans, src, g, n).reshape(n, 2 * chans, width)
         for j in range(n):
@@ -135,9 +157,16 @@
             slope = (1.0 - cand * cand) * skip
             maps_ref[row, 0] = rest * (1.0 - slope)
             maps_ref[row, 1] = rest * (cand - slope * guess)
-            fval = guess + rest * (cand - guess)
-            diff = shift_ref[row].astype(jnp.float32) - fval
-            total = total + diff * diff
+
+
+def residual_kernel(maps_ref, guess_ref, ahead_ref, res_ref):
+    rows, chans, width = guess_ref.shape
+    total = jnp.zeros((chans, width), jnp.float32)
+    for r in range(rows):
+        guess = guess_ref[r]
+        fval = guess - maps_ref[r, 0] * guess + maps_ref[r, 1]
+        diff = ahead_ref[r].astype(jnp.float32) - fval
+        total = total + diff * diff
     res_ref[...] = jnp.sum(total, axis=0, keepdims=True)
 
 
@@ -175,47 +204,68 @@
     flat = traj.reshape(chans * rows, width)
     begin = start_state.reshape(chans * rows, width)
 
-    shift, pair, chip = pl.pallas_call(
+    following = [
+        ((t + 1) % n_tm * n_space + s, t * n_space + s) for t in range(n_tm) for s in range(0, n_space, 2)
+    ]
+    act_next = lax.ppermute(actions, ("tm", "space"), following)
+    hbm = pl.BlockSpec(memory_space=pltpu.HBM)
+    vmem = pl.BlockSpec(memory_space=pltpu.VMEM)
+    own, pair, chip, guess, cols, line, proj = pl.pallas_call(
         send_kernel,
+        in_specs=[hbm] * 7 + [vmem],
         out_shape=(
-            jax.ShapeDtypeStruct((rows + 1, chans, width), bf16),
+            jax.ShapeDtypeStruct((rows, chans, width), bf16),
+            jax.ShapeDtypeStruct((HALO + 1, chans, width), bf16),
             jax.ShapeDtypeStruct((HALO, chans, width), bf16),
-            jax.ShapeDtypeStruct((HALO, chans, width), bf16),
+            jax.ShapeDtypeStruct((rows, chans, width), f32),
+            jax.ShapeDtypeStruct((6, chans, width), f32),
+            jax.ShapeDtypeStruct((chans, width), f32),
+            jax.ShapeDtypeStruct(act_proj.shape, f32),
         ),
-        scratch_shapes=[pltpu.VMEM((chans, width), f32)],
+        scratch_shapes=[
+            pltpu.VMEM((chans * rows, width), f32),
+            pltpu.VMEM((chans * rows, width), f32),
+            pltpu.VMEM(hidden_b.shape, f32),
+            pltpu.VMEM((1, chans), f32),
+            pltpu.VMEM((1, chans), f32),
+            pltpu.VMEM((1, chans), f32),
+            pltpu.SemaphoreType.DMA((7,)),
+        ],
         compiler_params=params(),
         name="sends",
-    )(flat, begin, actions)
-    shift = lax.ppermute(shift, "tm", [((t + 1) % n_tm, t) for t in range(n_tm)])
+    )(*[
+        pltpu.with_memory_space_constraint(value, pltpu.HBM)
+        for value in (flat, begin, hidden_b, cand_b[None], gate_b[None], skip[None], act_proj)
+    ], act_next)
     pair = lax.ppermute(pair, "space", [(s, s ^ 1) for s in range(n_space)])
     crossing = [(s, s + 1) for s in range(1, n_space - 1, 2)]
     chip = lax.ppermute(chip, "space", crossing + [(b, a) for a, b in crossing])
 
     kb = (GROUP + 2) * 128
-    maps, partial = pl.pallas_call(
+    maps = pl.pallas_call(
         conv_kernel,
-        out_shape=(
-            jax.ShapeDtypeStruct((rows, 2, chans, width), f32),
-            jax.ShapeDtypeStruct((1, width), f32),
-        ),
+        out_shape=jax.ShapeDtypeStruct((rows, 2, chans, width), f32),
         scratch_shapes=[
             pltpu.VMEM((rows + 2 * HALO, 128, width), bf16),
             pltpu.VMEM((rows + 2 * HALO, 128, width), bf16),
             pltpu.VMEM((GROUP * chans, kb), bf16),
             pltpu.VMEM((GROUP * 2 * chans, kb), bf16),
-            pltpu.VMEM((rows, chans, width), f32),
         ],
         compiler_params=params(),
         name="dynamics",
-    )(
-        shift, pair, chip, flat, begin, act_proj,
-        tap_rows(hidden_w, chans), hidden_b, tap_rows(head_w, 2 * chans),
-        cand_b[None], gate_b[None], skip[None],
-    )
+    )(guess, pair, chip, line, proj, cols, tap_rows(hidden_w, chans), tap_rows(head_w, 2 * chans))
 
     z_groups = [[x * NZ + z for z in range(NZ)] for x in range(NX)]
     x_groups = [[x * NZ + z for x in range(NX)] for z in range(NZ)]
     sent = lax.all_to_all(maps.astype(jnp.float16), "tm", 0, 0, axis_index_groups=z_groups)
+    ahead = lax.ppermute(own, "tm", [((t + 1) % n_tm, t) for t in range(n_tm)])
+    partial = pl.pallas_call(
+        residual_kernel,
+        out_shape=jax.ShapeDtypeStruct((1, width), f32),
+        compiler_params=params(),
+        cost_estimate=pl.CostEstimate(flops=2**19, bytes_accessed=2**20, transcendentals=0),
+        name="residual",
+    )(maps, guess, ahead)
     for bit in (1, 2):
         partial = partial + lax.ppermute(partial, "space", [(s, s ^ bit) for s in range(n_space)])
     sent, partial = lax.optimization_barrier((sent, partial))
@@ -242,9 +292,11 @@
         state = jnp.where(x < mine, blocks[x, 0] * state + blocks[x, 1], state)
     states = (pref[:, 0] * state + pref[:, 1]).astype(jnp.float16)
     back = lax.all_to_all(states, "tm", 0, 0, axis_index_groups=z_groups)
-    partial = partial + lax.ppermute(partial, "space", [(s, s ^ 4) for s in range(n_space)])
-    res_msq = jnp.sum(partial).reshape(1) / (chans * rows * width * n_space)
-    res_msq = lax.ppermute(res_msq, "tm", [(t, (t + 1) % n_tm) for t in range(n_tm)])
+    homes = []
+    for bit in (0, 4):
+        pairs = [(t * n_space + s, (t + 1) % n_tm * n_space + (s ^ bit)) for t in range(n_tm) for s in range(n_space)]
+        homes.append(lax.ppermute(partial, ("tm", "space"), pairs))
+    res_msq = jnp.sum(homes[0] + homes[1]).reshape(1) / (chans * rows * width * n_space)
     back, res_msq = lax.optimization_barrier((back, res_msq))
     new_traj = jnp.swapaxes(back.astype(f32), 0, 1)[None]
     return new_traj, res_msq

time: 88.8 us -> 99.7 us (1.12)
  the two profiles are of different devices: /device:TPU:8 before, /device:TPU:16 now
where the time goes in v3:
time: 99.7 us; the launch traced here: 99.1 us
  starting transfers between devices  56.3 us (56%)
  waiting for transfers between devices  30.8 us (31%)
  local copies, waits for them, and re-layouts  3.6 us (4%)
  Pallas kernels  3.52 us (4%)
  between operations  2.68 us (3%)
  other arithmetic  2.26 us (2%)
    ppermute x1, starting transfers between devices, body(): act_next = lax.ppermute(actions, ('tm', 'space'), following)  13.6 us
    all_to_all x1, starting transfers between devices, body(): back = lax.all_to_all(states, 'tm', 0, 0, axis_index_groups=z_groups)  10.6 us
    ppermute x1, waiting for transfers between devices, body(): ahead = lax.ppermute(own, 'tm', [((t + 1) % n_tm, t) for t in range(n_tm)])  9.75 us
    ppermute x2, waiting for transfers between devices, body(): homes.append(lax.ppermute(partial, ('tm', 'space'), pairs))  8.47 us
    ppermute x1, starting transfers between devices, body(): ahead = lax.ppermute(own, 'tm', [((t + 1) % n_tm, t) for t in range(n_tm)])  7.23 us
    ppermute x2, starting transfers between devices, body(): homes.append(lax.ppermute(partial, ('tm', 'space'), pairs))  6.53 us
    all_to_all x1, starting transfers between devices, body(): lax.all_to_all(maps.astype(jnp.float16), 'tm', 0, 0, axis_index_groups=z_...  5.78 us
    all_to_all x1, waiting for transfers between devices, body(): lax.all_to_all(jnp.broadcast_to(block[None], (NX,) + block.shape), 'tm',...  4.95 us
  transfers between devices with their start and end apart: 11, of which 8 were waited for; matrix products, arithmetic and copies ran while one was open for 2% of the time, Pallas kernels for 0%

profile of v3, /device:TPU:16, one launch (start us, length us, event | category | flops | bytes accessed | tf_op | source)
XLA Modules:
  0.0 99.1 jit_solution(6939316333729357094)
XLA Ops:
  0.6 13.6 %collective-permute-start = (f32[1,16]{1,0:T(1,128)}, f32[1,16]{1,0:T(1,128)S(1)}, u32[]{:S(2)}, u32[]{:S(2)}) collective-permute-start(f32[1,16]{1,0:T(1,128)} %param.12), channel_id=1, source_target_pairs={{8,0},{10,2},{12,4},{14,6},{16,8},{18,10},{20,12},{22,14},{24,16},... | collective-permute-start | bytes 200 | tf_op jit(solution)/shard_map/ppermute | solution.py:210
  14.2 1.4 %collective-permute-done.act_ref = f32[1,16]{1,0:T(1,128)S(1)} collective-permute-done((f32[1,16]{1,0:T(1,128)}, f32[1,16]{1,0:T(1,128)S(1)}, u32[]{:S(2)}, u32[]{:S(2)}) %collective-permute-start) | collective-permute-done | bytes 96 | tf_op jit(solution)/shard_map/ppermute | solution.py:210
  15.6 1.4 %sends.1 = (bf16[16,32,128]{2,1,0:T(8,128)(2,1)S(1)}, bf16[5,32,128]{2,1,0:T(8,128)(2,1)S(1)}, bf16[4,32,128]{2,1,0:T(8,128)(2,1)S(1)}, f32[16,32,128]{2,1,0:T(8...) custom-call(f32[512,128]{1,0:T(8,128)} %bitcast.174, f32[512,128]{1,0:T(8,128)} %bitcast.173, ...), custom_call_target="tpu_custom_call" | custom-call | tf_op jit(solution)/shard_map/sends/pallas_call | solution.py:213
  17.1 1.9 %collective-permute-start.1 = (bf16[5,32,128]{2,1,0:T(8,128)(2,1)S(1)}, bf16[5,32,128]{2,1,0:T(8,128)(2,1)S(1)}, u32[]{:S(2)}, u32[]{:S(2)}) collective-permute-start(bf16[5,32,128]{2,1,0:T(8,128)(2,1)S(1)} %get-tuple-element.14), channel_id=1, source_target_pairs={{0,1},{1,0},{2,3},{3,2},{4,5},{5,4},{6,7},{7,6},{8,9},{9,8},{10,11... | collective-permute-start | bytes 122888 | tf_op jit(solution)/shard_map/ppermute | solution.py:240
  19.0 2.5 %collective-permute-start.2 = (bf16[4,32,128]{2,1,0:T(8,128)(2,1)S(1)}, bf16[4,32,128]{2,1,0:T(8,128)(2,1)S(1)}, u32[]{:S(2)}, u32[]{:S(2)}) collective-permute-start(bf16[4,32,128]{2,1,0:T(8,128)(2,1)S(1)} %get-tuple-element.15), channel_id=1, source_target_pairs={{1,2},{3,4},{5,6},{2,1},{4,3},{6,5},{9,10},{11,12},{13,14},{10,9},... | collective-permute-start | bytes 98312 | tf_op jit(solution)/shard_map/ppermute | solution.py:242
  22.7 1.6 %collective-permute-done.2.chip_ref = bf16[4,32,128]{2,1,0:T(8,128)(2,1)S(1)} collective-permute-done((bf16[4,32,128]{2,1,0:T(8,128)(2,1)S(1)}, bf16[4,32,128]{2,1,0:T(8,128)(2,1)S(1)}, u32[]{:S(2)}, u32[]{:S(2)}) %collective-permute-start.2) | collective-permute-done | bytes 32800 | tf_op jit(solution)/shard_map/ppermute | solution.py:242
  24.2 2.0 %dynamics.1.maps_ref = f32[16,2,32,128]{3,2,1,0:T(8,128)S(1)} custom-call(f32[16,32,128]{2,1,0:T(8,128)S(1)} %get-tuple-element.13.guess_ref, bf16[5,32,128]{2,1,0:T(8,128)(2,1)S(1)} %collective-permute-done.1.pair_ref, bf16[4,32,128]{2,1,0:T(8,128)(2,1)S(1)} %collective-permute-done.2.chip_ref, f32[32,128]{1,0:T(8,128)S(1)} %get-tuple-element.16.line_ref, ...), custom_call_target="tpu_custom_call" | custom-call | tf_op jit(solution)/shard_map/dynamics/pallas_call | solution.py:245
  26.2 0.8 convert_element_type.454
  27.0 5.8 %all-to-all-start = ((f16[16,2,32,128]{3,2,1,0:T(8,128)(2,1)}), f16[16,2,32,128]{3,2,1,0:T(8,128)(2,1)S(1)}, u32[]{:S(2)}, u32[]{:S(2)}) async-start(f16[16,2,32,128]{3,2,1,0:T(8,128)(2,1)} %convert_element_type.454), calls=%async_computation | async-start | bytes 524288 | tf_op jit(solution)/shard_map/all_to_all | solution.py:260
  32.8 7.2 %collective-permute-start.3 = (bf16[16,32,128]{2,1,0:T(8,128)(2,1)S(1)}, bf16[16,32,128]{2,1,0:T(8,128)(2,1)S(1)}, u32[]{:S(2)}, u32[]{:S(2)}) collective-permute-start(bf16[16,32,128]{2,1,0:T(8,128)(2,1)S(1)} %get-tuple-element.19), channel_id=1, source_target_pairs={{8,0},{16,8},{24,16},{32,24},{40,32},{48,40},{56,48},{64,56},{72,6... | collective-permute-start | bytes 393224 | tf_op jit(solution)/shard_map/ppermute | solution.py:261
  40.0 9.8 %collective-permute-done.3.ahead_ref = bf16[16,32,128]{2,1,0:T(8,128)(2,1)S(1)} collective-permute-done((bf16[16,32,128]{2,1,0:T(8,128)(2,1)S(1)}, bf16[16,32,128]{2,1,0:T(8,128)(2,1)S(1)}, u32[]{:S(2)}, u32[]{:S(2)}) %collective-permute-start.3) | collective-permute-done | bytes 131104 | tf_op jit(solution)/shard_map/ppermute | solution.py:261
  49.9 1.9 %collective-permute-start.4 = (f32[1,128]{1,0:T(1,128)S(1)}, f32[1,128]{1,0:T(1,128)S(1)}, u32[]{:S(2)}, u32[]{:S(2)}) collective-permute-start(f32[1,128]{1,0:T(1,128)S(1)} %residual.1), channel_id=1, source_target_pairs={{0,1},{1,0},{2,3},{3,2},{4,5},{5,4},{6,7},{7,6},{8,9},{9,8},{10,11... | collective-permute-start | bytes 1544 | tf_op jit(solution)/shard_map/ppermute | solution.py:270
  51.8 1.1 %collective-permute-done.4 = f32[1,128]{1,0:T(1,128)S(1)} collective-permute-done((f32[1,128]{1,0:T(1,128)S(1)}, f32[1,128]{1,0:T(1,128)S(1)}, u32[]{:S(2)}, u32[]{:S(2)}) %collective-permute-start.4) | collective-permute-done | bytes 544 | tf_op jit(solution)/shard_map/ppermute | solution.py:270
  52.9 1.9 %collective-permute-start.5 = (f32[1,128]{1,0:T(1,128)S(1)}, f32[1,128]{1,0:T(1,128)S(1)}, u32[]{:S(2)}, u32[]{:S(2)}) collective-permute-start(f32[1,128]{1,0:T(1,128)S(1)} %add.206), channel_id=1, source_target_pairs={{0,2},{1,3},{2,0},{3,1},{4,6},{5,7},{6,4},{7,5},{8,10},{9,11},{10,... | collective-permute-start | bytes 1544 | tf_op jit(solution)/shard_map/ppermute | solution.py:270
  54.9 3.5 %collective-permute-done.5 = f32[1,128]{1,0:T(1,128)S(1)} collective-permute-done((f32[1,128]{1,0:T(1,128)S(1)}, f32[1,128]{1,0:T(1,128)S(1)}, u32[]{:S(2)}, u32[]{:S(2)}) %collective-permute-start.5) | collective-permute-done | bytes 544 | tf_op jit(solution)/shard_map/ppermute | solution.py:270
  59.2 4.3 %all-to-all-start.1 = ((f32[4,2,32,128]{3,2,1,0:T(8,128)}), f32[4,2,32,128]{3,2,1,0:T(8,128)S(1)}, u32[]{:S(2)}, u32[]{:S(2)}) async-start(f32[4,2,32,128]{3,2,1,0:T(8,128)} %broadcast_in_dim.25), calls=%async_computation.1 | async-start | bytes 262144 | tf_op jit(solution)/shard_map/all_to_all | solution.py:279
  63.5 0.9 constant_dynamic-slice_fusion
  64.5 4.9 %all-to-all-done.1 = f32[4,2,32,128]{3,2,1,0:T(8,128)S(1)} async-done(((f32[4,2,32,128]{3,2,1,0:T(8,128)}), f32[4,2,32,128]{3,2,1,0:T(8,128)S(1)}, u32[]{:S(2)}, u32[]{:S(2)}) %all-to-all-start.1) | async-done | bytes 131104 | tf_op jit(solution)/shard_map/all_to_all | solution.py:279
  70.1 10.6 %all-to-all-start.2 = ((f16[16,32,128]{2,1,0:T(8,128)(2,1)}), f16[16,32,128]{2,1,0:T(8,128)(2,1)S(1)}, u32[]{:S(2)}, u32[]{:S(2)}) async-start(f16[16,32,128]{2,1,0:T(8,128)(2,1)} %fusion.1), calls=%async_computation.2 | async-start | bytes 262144 | tf_op jit(solution)/shard_map/all_to_all | solution.py:294
  80.8 3.8 %collective-permute-start.6 = (f32[1,128]{1,0:T(1,128)S(1)}, f32[1,128]{1,0:T(1,128)S(1)}, u32[]{:S(2)}, u32[]{:S(2)}) collective-permute-start(f32[1,128]{1,0:T(1,128)S(1)} %add.207), channel_id=1, source_target_pairs={{0,8},{1,9},{2,10},{3,11},{4,12},{5,13},{6,14},{7,15},{8,16},{9,17... | collective-permute-start | bytes 1544 | tf_op jit(solution)/shard_map/ppermute | solution.py:298
  84.6 2.7 %collective-permute-start.7 = (f32[1,128]{1,0:T(1,128)S(1)}, f32[1,128]{1,0:T(1,128)S(1)}, u32[]{:S(2)}, u32[]{:S(2)}) collective-permute-start(f32[1,128]{1,0:T(1,128)S(1)} %add.207), channel_id=1, source_target_pairs={{0,12},{1,13},{2,14},{3,15},{4,8},{5,9},{6,10},{7,11},{8,20},{9,21... | collective-permute-start | bytes 1544 | tf_op jit(solution)/shard_map/ppermute | solution.py:298
  87.3 2.2 %collective-permute-done.6 = f32[1,128]{1,0:T(1,128)S(1)} collective-permute-done((f32[1,128]{1,0:T(1,128)S(1)}, f32[1,128]{1,0:T(1,128)S(1)}, u32[]{:S(2)}, u32[]{:S(2)}) %collective-permute-start.6) | collective-permute-done | bytes 544 | tf_op jit(solution)/shard_map/ppermute | solution.py:298
  89.6 6.2 %collective-permute-done.7 = f32[1,128]{1,0:T(1,128)S(1)} collective-permute-done((f32[1,128]{1,0:T(1,128)S(1)}, f32[1,128]{1,0:T(1,128)S(1)}, u32[]{:S(2)}, u32[]{:S(2)}) %collective-permute-start.7) | collective-permute-done | bytes 544 | tf_op jit(solution)/shard_map/ppermute | solution.py:298
  97.1 0.9 copy.19
  (25 shorter events, 3.4 us)
Async XLA Ops:
  0.6 15.0 %collective-permute-start = (f32[1,16]{1,0:T(1,128)}, f32[1,16]{1,0:T(1,128)S(1)}, u32[]{:S(2)}, u32[]{:S(2)}) collective-permute-start(f32[1,16]{1,0:T(1,128)} %param.12), channel_id=1, source_target_pairs={{8,0},{10,2},{12,4},{14,6},{16,8},{18,10},{20,12},{22,14},{24,16},... | collective-permute-start | bytes 200 | tf_op jit(solution)/shard_map/ppermute | solution.py:210
  15.6 5.8 %copy-start = (bf16[3,9,32,32]{3,2,1,0:T(8,128)(2,1)S(1)}, bf16[3,9,32,32]{3,2,1,0:T(8,128)(2,1)}, u32[]{:S(2)}) copy-start(bf16[3,9,32,32]{3,2,1,0:T(8,128)(2,1)} %param.13) | copy-start | bytes 165892
  17.1 7.2 %collective-permute-start.1 = (bf16[5,32,128]{2,1,0:T(8,128)(2,1)S(1)}, bf16[5,32,128]{2,1,0:T(8,128)(2,1)S(1)}, u32[]{:S(2)}, u32[]{:S(2)}) collective-permute-start(bf16[5,32,128]{2,1,0:T(8,128)(2,1)S(1)} %get-tuple-element.14), channel_id=1, source_target_pairs={{0,1},{1,0},{2,3},{3,2},{4,5},{5,4},{6,7},{7,6},{8,9},{9,8},{10,11... | collective-permute-start | bytes 122888 | tf_op jit(solution)/shard_map/ppermute | solution.py:240
  19.0 5.2 %collective-permute-start.2 = (bf16[4,32,128]{2,1,0:T(8,128)(2,1)S(1)}, bf16[4,32,128]{2,1,0:T(8,128)(2,1)S(1)}, u32[]{:S(2)}, u32[]{:S(2)}) collective-permute-start(bf16[4,32,128]{2,1,0:T(8,128)(2,1)S(1)} %get-tuple-element.15), channel_id=1, source_target_pairs={{1,2},{3,4},{5,6},{2,1},{4,3},{6,5},{9,10},{11,12},{13,14},{10,9},... | collective-permute-start | bytes 98312 | tf_op jit(solution)/shard_map/ppermute | solution.py:242
  21.6 0.9 copy-start.1
  27.0 31.4 %all-to-all-start = ((f16[16,2,32,128]{3,2,1,0:T(8,128)(2,1)}), f16[16,2,32,128]{3,2,1,0:T(8,128)(2,1)S(1)}, u32[]{:S(2)}, u32[]{:S(2)}) async-start(f16[16,2,32,128]{3,2,1,0:T(8,128)(2,1)} %convert_element_type.454), calls=%async_computation | async-start | bytes 524288 | tf_op jit(solution)/shard_map/all_to_all | solution.py:260
  32.8 17.0 %collective-permute-start.3 = (bf16[16,32,128]{2,1,0:T(8,128)(2,1)S(1)}, bf16[16,32,128]{2,1,0:T(8,128)(2,1)S(1)}, u32[]{:S(2)}, u32[]{:S(2)}) collective-permute-start(bf16[16,32,128]{2,1,0:T(8,128)(2,1)S(1)} %get-tuple-element.19), channel_id=1, source_target_pairs={{8,0},{16,8},{24,16},{32,24},{40,32},{48,40},{56,48},{64,56},{72,6... | collective-permute-start | bytes 393224 | tf_op jit(solution)/shard_map/ppermute | solution.py:261
  49.9 3.1 %collective-permute-start.4 = (f32[1,128]{1,0:T(1,128)S(1)}, f32[1,128]{1,0:T(1,128)S(1)}, u32[]{:S(2)}, u32[]{:S(2)}) collective-permute-start(f32[1,128]{1,0:T(1,128)S(1)} %residual.1), channel_id=1, source_target_pairs={{0,1},{1,0},{2,3},{3,2},{4,5},{5,4},{6,7},{7,6},{8,9},{9,8},{10,11... | collective-permute-start | bytes 1544 | tf_op jit(solution)/shard_map/ppermute | solution.py:270
  52.9 5.5 %collective-permute-start.5 = (f32[1,128]{1,0:T(1,128)S(1)}, f32[1,128]{1,0:T(1,128)S(1)}, u32[]{:S(2)}, u32[]{:S(2)}) collective-permute-start(f32[1,128]{1,0:T(1,128)S(1)} %add.206), channel_id=1, source_target_pairs={{0,2},{1,3},{2,0},{3,1},{4,6},{5,7},{6,4},{7,5},{8,10},{9,11},{10,... | collective-permute-start | bytes 1544 | tf_op jit(solution)/shard_map/ppermute | solution.py:270
  59.2 10.3 %all-to-all-start.1 = ((f32[4,2,32,128]{3,2,1,0:T(8,128)}), f32[4,2,32,128]{3,2,1,0:T(8,128)S(1)}, u32[]{:S(2)}, u32[]{:S(2)}) async-start(f32[4,2,32,128]{3,2,1,0:T(8,128)} %broadcast_in_dim.25), calls=%async_computation.1 | async-start | bytes 262144 | tf_op jit(solution)/shard_map/all_to_all | solution.py:279
  70.1 26.9 %all-to-all-start.2 = ((f16[16,32,128]{2,1,0:T(8,128)(2,1)}), f16[16,32,128]{2,1,0:T(8,128)(2,1)S(1)}, u32[]{:S(2)}, u32[]{:S(2)}) async-start(f16[16,32,128]{2,1,0:T(8,128)(2,1)} %fusion.1), calls=%async_computation.2 | async-start | bytes 262144 | tf_op jit(solution)/shard_map/all_to_all | solution.py:294
  80.8 8.8 %collective-permute-start.6 = (f32[1,128]{1,0:T(1,128)S(1)}, f32[1,128]{1,0:T(1,128)S(1)}, u32[]{:S(2)}, u32[]{:S(2)}) collective-permute-start(f32[1,128]{1,0:T(1,128)S(1)} %add.207), channel_id=1, source_target_pairs={{0,8},{1,9},{2,10},{3,11},{4,12},{5,13},{6,14},{7,15},{8,16},{9,17... | collective-permute-start | bytes 1544 | tf_op jit(solution)/shard_map/ppermute | solution.py:298
  84.6 11.2 %collective-permute-start.7 = (f32[1,128]{1,0:T(1,128)S(1)}, f32[1,128]{1,0:T(1,128)S(1)}, u32[]{:S(2)}, u32[]{:S(2)}) collective-permute-start(f32[1,128]{1,0:T(1,128)S(1)} %add.207), channel_id=1, source_target_pairs={{0,12},{1,13},{2,14},{3,15},{4,8},{5,9},{6,10},{7,11},{8,20},{9,21... | collective-permute-start | bytes 1544 | tf_op jit(solution)/shard_map/ppermute | solution.py:298

commit v4 on v3

--- a/solution.py
+++ b/solution.py
@@ -29,23 +29,25 @@
 
 
 def send_kernel(
-    traj_hbm, start_hbm, hb_hbm, cb_hbm, gb_hbm, sk_hbm, proj_hbm, act_ref,
-    own_ref, pair_ref, chip_ref, guess_ref, cols_ref, line_ref, proj_ref,
-    traj_ref, start_ref, hb_ref, cb_ref, gb_ref, sk_ref, sems,
+    traj_hbm, start_hbm, act_hbm, hb_hbm, cb_hbm, gb_hbm, sk_hbm, proj_hbm, wh_hbm, wo_hbm,
+    shift_ref, pair_ref, chip_ref, guess_ref, begin_ref, cols_ref, proj_ref, th_ref, to_ref,
+    traj_ref, start_ref, act_ref, hb_ref, cb_ref, gb_ref, sk_ref, wh_ref, wo_ref, line_ref, sems,
 ):
-    chans, width = own_ref.shape[1:]
-    rows = own_ref.shape[0]
+    rows, chans, width = guess_ref.shape
     moves = [
         pltpu.make_async_copy(source, target, sems.at[i])
         for i, (source, target) in enumerate(
             (
                 (traj_hbm, traj_ref),
                 (start_hbm, start_ref),
+                (act_hbm, act_ref),
                 (hb_hbm, hb_ref),
                 (cb_hbm, cb_ref),
                 (gb_hbm, gb_ref),
                 (sk_hbm, sk_ref),
                 (proj_hbm, proj_ref),
+                (wh_hbm, wh_ref),
+                (wo_hbm, wo_ref),
             )
         )
     ]
@@ -54,14 +56,14 @@
     last = lax.axis_index("tm") == lax.axis_size("tm") - 1
     even = lax.rem(lax.axis_index("space"), 2) == 0
     line_ref[...] = jnp.zeros(line_ref.shape, jnp.float32)
+    for move in moves:
+        move.wait()
     rest = act_ref[...]
     for part in range(3):
         piece = rounded(rest)
         line_ref[part : part + 1, : piece.shape[1]] = piece
         rest = rest - piece
-    pair_ref[HALO] = line_ref[...].astype(jnp.bfloat16)
-    for move in moves:
-        move.wait()
+    shift_ref[rows] = line_ref[...].astype(jnp.bfloat16)
 
     def spread(vec):
         return jnp.broadcast_to(column(vec), (chans, width))
@@ -74,17 +76,29 @@
     for r in range(rows):
         at = pl.ds(r, chans, stride=rows)
         mine = traj_ref[at, :]
-        own_ref[r] = mine.astype(jnp.bfloat16)
+        shift_ref[r] = mine.astype(jnp.bfloat16)
         guess_ref[r] = jnp.where(last, start_ref[at, :], mine)
+    place = lax.rem(lax.axis_index("tm"), NZ)
+    begin_ref[...] = start_ref[pl.ds(place, chans, stride=rows), :]
     for r in range(HALO):
         upper, lower = guess_ref[r], guess_ref[rows - HALO + r]
         pair_ref[r] = jnp.where(even, lower, upper).astype(jnp.bfloat16)
         chip_ref[r] = jnp.where(even, upper, lower).astype(jnp.bfloat16)
+    for a in range(3):
+        for layer in range(3):
+            th_ref[layer, a] = tile_of([wh_ref[layer, 3 * a + b].astype(jnp.float32) for b in range(3)])
+        to_ref[a] = tile_of([wo_ref[3 * a + b].astype(jnp.float32).T for b in range(3)])
+
+
+def tile_of(taps):
+    outs, chans = taps[0].shape
+    pad = jnp.zeros((outs, 128 - 3 * chans), jnp.float32)
+    return jnp.concatenate(taps + [pad], axis=1).astype(jnp.bfloat16)
 
 
 def conv_kernel(
-    guess_ref, pair_ref, chip_ref, line_ref, proj_ref, cols_ref, wh_ref, wo_ref,
-    maps_ref, xa_ref, xb_ref, band_ref, head_ref,
+    guess_ref, shift_ref, pair_ref, chip_ref, proj_ref, cols_ref, wh_ref, wo_ref,
+    maps_ref, res_ref, xa_ref, xb_ref, band_ref, head_ref,
 ):
     strip = lax.axis_index("space")
     even = lax.rem(strip, 2) == 0
@@ -97,7 +111,7 @@
     band_ref[...] = jnp.zeros(band_ref.shape, jnp.bfloat16)
     head_ref[...] = jnp.zeros(head_ref.shape, jnp.bfloat16)
 
-    parts = jnp.where(even, line_ref[...], pair_ref[HALO].astype(jnp.float32))
+    parts = shift_ref[rows].astype(jnp.float32)
     line = parts[0:1] + parts[1:2] + parts[2:3]
     act = column(line[:, : proj_ref.shape[0]])
     terms = jnp.sum(act * proj_ref[...], axis=0, keepdims=True)
@@ -147,6 +161,7 @@
     for r in range(GROUP):
         for a in range(3):
             head_ref[r * 2 * chans : (r + 1) * 2 * chans, (r + a) * 128 : (r + a + 1) * 128] = wo_ref[a]
+    total = jnp.zeros((chans, width), jnp.float32)
     for g, n in groups_of(rows):
         acc = product(head_ref, 2 * chans, src, g, n).reshape(n, 2 * chans, width)
         for j in range(n):
@@ -157,16 +172,9 @@
             slope = (1.0 - cand * cand) * skip
             maps_ref[row, 0] = rest * (1.0 - slope)
             maps_ref[row, 1] = rest * (cand - slope * guess)
-
-
-def residual_kernel(maps_ref, guess_ref, ahead_ref, res_ref):
-    rows, chans, width = guess_ref.shape
-    total = jnp.zeros((chans, width), jnp.float32)
-    for r in range(rows):
-        guess = guess_ref[r]
-        fval = guess - maps_ref[r, 0] * guess + maps_ref[r, 1]
-        diff = ahead_ref[r].astype(jnp.float32) - fval
-        total = total + diff * diff
+            fval = guess + rest * (cand - guess)
+            diff = shift_ref[row].astype(jnp.float32) - fval
+            total = total + diff * diff
     res_ref[...] = jnp.sum(total, axis=0, keepdims=True)
 
 
@@ -183,14 +191,6 @@
         a, b = keep * a, keep * b + maps_ref[z, 1]
 
 
-def tap_rows(weights, outs):
-    lead = weights.shape[:-3]
-    chans = weights.shape[-1]
-    split = weights.reshape(lead + (3, 3, outs, chans))
-    moved = jnp.swapaxes(split, -3, -2).reshape(lead + (3, outs, 3 * chans))
-    return jnp.pad(moved, [(0, 0)] * (len(lead) + 2) + [(0, 128 - 3 * chans)])
-
-
 def params():
     return pltpu.CompilerParams(vmem_limit_bytes=LIMIT)
 
@@ -204,47 +204,51 @@
     flat = traj.reshape(chans * rows, width)
     begin = start_state.reshape(chans * rows, width)
 
-    following = [
-        ((t + 1) % n_tm * n_space + s, t * n_space + s) for t in range(n_tm) for s in range(0, n_space, 2)
-    ]
-    act_next = lax.ppermute(actions, ("tm", "space"), following)
-    hbm = pl.BlockSpec(memory_space=pltpu.HBM)
-    vmem = pl.BlockSpec(memory_space=pltpu.VMEM)
-    own, pair, chip, guess, cols, line, proj = pl.pallas_call(
+    loaded = (
+        flat, begin, actions, hidden_b, cand_b[None], gate_b[None], skip[None], act_proj, hidden_w, jnp.swapaxes(head_w, 1, 2),
+    )
+    shift, pair, chip, guess, entry, cols, proj, taps, head_taps = pl.pallas_call(
         send_kernel,
-        in_specs=[hbm] * 7 + [vmem],
+        in_specs=[pl.BlockSpec(memory_space=pltpu.HBM)] * len(loaded),
         out_shape=(
-            jax.ShapeDtypeStruct((rows, chans, width), bf16),
-            jax.ShapeDtypeStruct((HALO + 1, chans, width), bf16),
+            jax.ShapeDtypeStruct((rows + 1, chans, width), bf16),
+            jax.ShapeDtypeStruct((HALO, chans, width), bf16),
             jax.ShapeDtypeStruct((HALO, chans, width), bf16),
             jax.ShapeDtypeStruct((rows, chans, width), f32),
+            jax.ShapeDtypeStruct((chans, width), f32),
             jax.ShapeDtypeStruct((6, chans, width), f32),
-            jax.ShapeDtypeStruct((chans, width), f32),
             jax.ShapeDtypeStruct(act_proj.shape, f32),
+            jax.ShapeDtypeStruct((3, 3, chans, 128), bf16),
+            jax.ShapeDtypeStruct((3, 2 * chans, 128), bf16),
         ),
         scratch_shapes=[
             pltpu.VMEM((chans * rows, width), f32),
             pltpu.VMEM((chans * rows, width), f32),
+            pltpu.VMEM(actions.shape, f32),
             pltpu.VMEM(hidden_b.shape, f32),
             pltpu.VMEM((1, chans), f32),
             pltpu.VMEM((1, chans), f32),
             pltpu.VMEM((1, chans), f32),
-            pltpu.SemaphoreType.DMA((7,)),
+            pltpu.VMEM(hidden_w.shape, bf16),
+            pltpu.VMEM((9, chans, 2 * chans), bf16),
+            pltpu.VMEM((chans, width), f32),
+            pltpu.SemaphoreType.DMA((len(loaded),)),
         ],
         compiler_params=params(),
         name="sends",
-    )(*[
-        pltpu.with_memory_space_constraint(value, pltpu.HBM)
-        for value in (flat, begin, hidden_b, cand_b[None], gate_b[None], skip[None], act_proj)
-    ], act_next)
+    )(*[pltpu.with_memory_space_constraint(value, pltpu.HBM) for value in loaded])
+    crossing = [(s, s + 1) for s in range(1, n_space - 1, 2)]
+    shift = lax.ppermute(shift, "tm", [((t + 1) % n_tm, t) for t in range(n_tm)])
+    chip = lax.ppermute(chip, "space", crossing + [(b, a) for a, b in crossing])
     pair = lax.ppermute(pair, "space", [(s, s ^ 1) for s in range(n_space)])
-    crossing = [(s, s + 1) for s in range(1, n_space - 1, 2)]
-    chip = lax.ppermute(chip, "space", crossing + [(b, a) for a, b in crossing])
 
     kb = (GROUP + 2) * 128
-    maps = pl.pallas_call(
+    maps, partial = pl.pallas_call(
         conv_kernel,
-        out_shape=jax.ShapeDtypeStruct((rows, 2, chans, width), f32),
+        out_shape=(
+            jax.ShapeDtypeStruct((rows, 2, chans, width), f32),
+            jax.ShapeDtypeStruct((1, width), f32),
+        ),
         scratch_shapes=[
             pltpu.VMEM((rows + 2 * HALO, 128, width), bf16),
             pltpu.VMEM((rows + 2 * HALO, 128, width), bf16),
@@ -253,32 +257,22 @@
         ],
         compiler_params=params(),
         name="dynamics",
-    )(guess, pair, chip, line, proj, cols, tap_rows(hidden_w, chans), tap_rows(head_w, 2 * chans))
+    )(guess, shift, pair, chip, proj, cols, taps, head_taps)
 
     z_groups = [[x * NZ + z for z in range(NZ)] for x in range(NX)]
     x_groups = [[x * NZ + z for x in range(NX)] for z in range(NZ)]
     sent = lax.all_to_all(maps.astype(jnp.float16), "tm", 0, 0, axis_index_groups=z_groups)
-    ahead = lax.ppermute(own, "tm", [((t + 1) % n_tm, t) for t in range(n_tm)])
-    partial = pl.pallas_call(
-        residual_kernel,
-        out_shape=jax.ShapeDtypeStruct((1, width), f32),
-        compiler_params=params(),
-        cost_estimate=pl.CostEstimate(flops=2**19, bytes_accessed=2**20, transcendentals=0),
-        name="residual",
-    )(maps, guess, ahead)
-    for bit in (1, 2):
+    for bit in (1, 2, 4):
         partial = partial + lax.ppermute(partial, "space", [(s, s ^ bit) for s in range(n_space)])
-    sent, partial = lax.optimization_barrier((sent, partial))
+    res_msq = jnp.sum(partial).reshape(1) / (chans * rows * width * n_space)
+    flags = [mine == NX - 1] + [x < mine for x in range(NX - 1)]
+    sent, res_msq, flags = lax.optimization_barrier((sent, res_msq, flags))
 
     steps = [(1.0 - sent[z, 0].astype(f32), sent[z, 1].astype(f32)) for z in range(NZ)]
     block_a, block_b = steps[0]
     for a, b in steps[1:]:
         block_a, block_b = a * block_a, a * block_b + b
-    final = mine == NX - 1
-    block = jnp.stack([jnp.where(final, steps[-1][0], block_a), jnp.where(final, steps[-1][1], block_b)])
-    blocks = lax.all_to_all(
-        jnp.broadcast_to(block[None], (NX,) + block.shape), "tm", 0, 0, axis_index_groups=x_groups
-    )
+    block = jnp.stack([jnp.where(flags[0], steps[-1][0], block_a), jnp.where(flags[0], steps[-1][1], block_b)])
     pref = pl.pallas_call(
         prefix_kernel,
         out_shape=jax.ShapeDtypeStruct((NZ, 2, chans, width), f32),
@@ -286,17 +280,14 @@
         cost_estimate=pl.CostEstimate(flops=2**20, bytes_accessed=2**20, transcendentals=0),
         name="prefix",
     )(sent.astype(f32))
-    state = lax.dynamic_index_in_dim(start_state, place % NZ, 1, False)
-    state = blocks[NX - 1, 0] * state + blocks[NX - 1, 1]
+    copies, pref, entry = lax.optimization_barrier((jnp.broadcast_to(block[None], (NX,) + block.shape), pref, entry))
+    blocks = lax.all_to_all(copies, "tm", 0, 0, axis_index_groups=x_groups)
+    state = blocks[NX - 1, 0] * entry + blocks[NX - 1, 1]
     for x in range(NX - 1):
-        state = jnp.where(x < mine, blocks[x, 0] * state + blocks[x, 1], state)
+        state = jnp.where(flags[x + 1], blocks[x, 0] * state + blocks[x, 1], state)
     states = (pref[:, 0] * state + pref[:, 1]).astype(jnp.float16)
     back = lax.all_to_all(states, "tm", 0, 0, axis_index_groups=z_groups)
-    homes = []
-    for bit in (0, 4):
-        pairs = [(t * n_space + s, (t + 1) % n_tm * n_space + (s ^ bit)) for t in range(n_tm) for s in range(n_space)]
-        homes.append(lax.ppermute(partial, ("tm", "space"), pairs))
-    res_msq = jnp.sum(homes[0] + homes[1]).reshape(1) / (chans * rows * width * n_space)
+    res_msq = lax.ppermute(res_msq, "tm", [(t, (t + 1) % n_tm) for t in range(n_tm)])
     back, res_msq = lax.optimization_barrier((back, res_msq))
     new_traj = jnp.swapaxes(back.astype(f32), 0, 1)[None]
     return new_traj, res_msq

time: 99.7 us -> 86.1 us (0.86)
  the two profiles are of different devices: /device:TPU:16 before, /device:TPU:24 now
where the time goes in v4:
time: 86.1 us; the launch traced here: 85.6 us
  starting transfers between devices  47.1 us (55%)
  waiting for transfers between devices  18.2 us (21%)
  blocking collectives  10.1 us (12%)
  Pallas kernels  3.8 us (4%)
  between operations  3.23 us (4%)
  other arithmetic  2.26 us (3%)
  local copies, waits for them, and re-layouts  0.87 us (1%)
    ppermute x1, starting transfers between devices, body(): lax.ppermute(shift, 'tm', [((t + 1) % n_tm, t) for t in range(n_tm)])  13.6 us
    all_to_all x1, starting transfers between devices, body(): back = lax.all_to_all(states, 'tm', 0, 0, axis_index_groups=z_groups)  12 us
    all_to_all x1, blocking collectives, body(): blocks = lax.all_to_all(copies, 'tm', 0, 0, axis_index_groups=x_groups)  10.1 us
    ppermute x3, waiting for transfers between devices, body(): lax.ppermute(partial, 'space', [(s, s ^ bit) for s in range(n_space)])  7.73 us
    ppermute x3, starting transfers between devices, body(): lax.ppermute(partial, 'space', [(s, s ^ bit) for s in range(n_space)])  7.67 us
    ppermute x1, starting transfers between devices, body(): lax.ppermute(res_msq, 'tm', [(t, (t + 1) % n_tm) for t in range(n_tm)])  5.11 us
    all_to_all x1, waiting for transfers between devices, body(): back = lax.all_to_all(states, 'tm', 0, 0, axis_index_groups=z_groups)  4.21 us
    all_to_all x1, starting transfers between devices, body(): lax.all_to_all(maps.astype(jnp.float16), 'tm', 0, 0, axis_index_groups=z_...  4.09 us
  transfers between devices with their start and end apart: 9, of which 6 were waited for; matrix products, arithmetic and copies ran while one was open for 1% of the time, Pallas kernels for 0%

profile of v4, /device:TPU:24, one launch (start us, length us, event | category | flops | bytes accessed | tf_op | source)
XLA Modules:
  0.0 85.6 jit_solution(12535186236831410909)
XLA Ops:
  0.6 1.7 %sends.1 = (bf16[17,32,128]{2,1,0:T(8,128)(2,1)S(1)}, bf16[4,32,128]{2,1,0:T(8,128)(2,1)S(1)}, bf16[4,32,128]{2,1,0:T(8,128)(2,1)S(1)}, f32[16,32,128]{2,1,0:T(8...) custom-call(f32[512,128]{1,0:T(8,128)} %bitcast.159, ...), custom_call_target="tpu_custom_call" | custom-call | tf_op jit(solution)/shard_map/sends/pallas_call | solution.py:210
  2.4 13.6 %collective-permute-start = (bf16[17,32,128]{2,1,0:T(8,128)(2,1)S(1)}, bf16[17,32,128]{2,1,0:T(8,128)(2,1)S(1)}, u32[]{:S(2)}, u32[]{:S(2)}) collective-permute-start(bf16[17,32,128]{2,1,0:T(8,128)(2,1)S(1)} %get-tuple-element.25), channel_id=1, source_target_pairs={{8,0},{16,8},{24,16},{32,24},{40,32},{48,40},{56,48},{64,56},{72,6... | collective-permute-start | bytes 417800 | tf_op jit(solution)/shard_map/ppermute | solution.py:241
  16.0 1.9 %collective-permute-start.1 = (bf16[4,32,128]{2,1,0:T(8,128)(2,1)S(1)}, bf16[4,32,128]{2,1,0:T(8,128)(2,1)S(1)}, u32[]{:S(2)}, u32[]{:S(2)}) collective-permute-start(bf16[4,32,128]{2,1,0:T(8,128)(2,1)S(1)} %get-tuple-element.26), channel_id=1, source_target_pairs={{0,1},{1,0},{2,3},{3,2},{4,5},{5,4},{6,7},{7,6},{8,9},{9,8},{10,11... | collective-permute-start | bytes 98312 | tf_op jit(solution)/shard_map/ppermute | solution.py:243
  17.9 2.8 %collective-permute-start.2 = (bf16[4,32,128]{2,1,0:T(8,128)(2,1)S(1)}, bf16[4,32,128]{2,1,0:T(8,128)(2,1)S(1)}, u32[]{:S(2)}, u32[]{:S(2)}) collective-permute-start(bf16[4,32,128]{2,1,0:T(8,128)(2,1)S(1)} %get-tuple-element.27), channel_id=1, source_target_pairs={{1,2},{3,4},{5,6},{2,1},{4,3},{6,5},{9,10},{11,12},{13,14},{10,9},... | collective-permute-start | bytes 98312 | tf_op jit(solution)/shard_map/ppermute | solution.py:242
  20.7 2.5 %collective-permute-done.2.chip_ref = bf16[4,32,128]{2,1,0:T(8,128)(2,1)S(1)} collective-permute-done((bf16[4,32,128]{2,1,0:T(8,128)(2,1)S(1)}, bf16[4,32,128]{2,1,0:T(8,128)(2,1)S(1)}, u32[]{:S(2)}, u32[]{:S(2)}) %collective-permute-start.2) | collective-permute-done | bytes 32800 | tf_op jit(solution)/shard_map/ppermute | solution.py:242
  23.1 2.0 %dynamics.1 = (f32[16,2,32,128]{3,2,1,0:T(8,128)S(1)}, f32[1,128]{1,0:T(1,128)S(1)}) custom-call(f32[16,32,128]{2,1,0:T(8,128)S(1)} %get-tuple-element.24.guess_ref, bf16[17,32,128]{2,1,0:T(8,128)(2,1)S(1)} %collective-permute-done.shift_ref, bf16[4,32,128]{2,1,0:T(8,128)(2,1)S(1)} %collective-permute-done.1.pair_ref, ...), custom_call_target="tpu_custom_call" | custom-call | tf_op jit(solution)/shard_map/dynamics/pallas_call | solution.py:246
  25.2 0.8 convert_element_type.450
  25.9 4.1 %all-to-all-start = ((f16[16,2,32,128]{3,2,1,0:T(8,128)(2,1)}), f16[16,2,32,128]{3,2,1,0:T(8,128)(2,1)S(1)}, u32[]{:S(2)}, u32[]{:S(2)}) async-start(f16[16,2,32,128]{3,2,1,0:T(8,128)(2,1)} %convert_element_type.450), calls=%async_computation | async-start | bytes 524288 | tf_op jit(solution)/shard_map/all_to_all | solution.py:264
  30.0 1.9 %collective-permute-start.3 = (f32[1,128]{1,0:T(1,128)S(1)}, f32[1,128]{1,0:T(1,128)S(1)}, u32[]{:S(2)}, u32[]{:S(2)}) collective-permute-start(f32[1,128]{1,0:T(1,128)S(1)} %get-tuple-element.33), channel_id=1, source_target_pairs={{0,1},{1,0},{2,3},{3,2},{4,5},{5,4},{6,7},{7,6},{8,9},{9,8},{10,11... | collective-permute-start | bytes 1544 | tf_op jit(solution)/shard_map/ppermute | solution.py:266
  32.0 1.1 %collective-permute-done.3 = f32[1,128]{1,0:T(1,128)S(1)} collective-permute-done((f32[1,128]{1,0:T(1,128)S(1)}, f32[1,128]{1,0:T(1,128)S(1)}, u32[]{:S(2)}, u32[]{:S(2)}) %collective-permute-start.3) | collective-permute-done | bytes 544 | tf_op jit(solution)/shard_map/ppermute | solution.py:266
  33.1 2.6 %collective-permute-start.4 = (f32[1,128]{1,0:T(1,128)S(1)}, f32[1,128]{1,0:T(1,128)S(1)}, u32[]{:S(2)}, u32[]{:S(2)}) collective-permute-start(f32[1,128]{1,0:T(1,128)S(1)} %add.178), channel_id=1, source_target_pairs={{0,2},{1,3},{2,0},{3,1},{4,6},{5,7},{6,4},{7,5},{8,10},{9,11},{10,... | collective-permute-start | bytes 1544 | tf_op jit(solution)/shard_map/ppermute | solution.py:266
  35.7 2.8 %collective-permute-done.4 = f32[1,128]{1,0:T(1,128)S(1)} collective-permute-done((f32[1,128]{1,0:T(1,128)S(1)}, f32[1,128]{1,0:T(1,128)S(1)}, u32[]{:S(2)}, u32[]{:S(2)}) %collective-permute-start.4) | collective-permute-done | bytes 544 | tf_op jit(solution)/shard_map/ppermute | solution.py:266
  38.5 3.1 %collective-permute-start.5 = (f32[1,128]{1,0:T(1,128)S(1)}, f32[1,128]{1,0:T(1,128)S(1)}, u32[]{:S(2)}, u32[]{:S(2)}) collective-permute-start(f32[1,128]{1,0:T(1,128)S(1)} %add.179), channel_id=1, source_target_pairs={{0,4},{1,5},{2,6},{3,7},{4,0},{5,1},{6,2},{7,3},{8,12},{9,13},{10,... | collective-permute-start | bytes 1544 | tf_op jit(solution)/shard_map/ppermute | solution.py:266
  41.7 3.8 %collective-permute-done.5 = f32[1,128]{1,0:T(1,128)S(1)} collective-permute-done((f32[1,128]{1,0:T(1,128)S(1)}, f32[1,128]{1,0:T(1,128)S(1)}, u32[]{:S(2)}, u32[]{:S(2)}) %collective-permute-start.5) | collective-permute-done | bytes 544 | tf_op jit(solution)/shard_map/ppermute | solution.py:266
  45.5 0.6 add_reduce_fusion
  46.8 0.1 add_select_fusion
  46.9 0.1 convert_element_type.497.maps_ref
  47.0 10.1 %all_to_all.15 = f32[4,2,32,128]{3,2,1,0:T(8,128)S(1)} all-to-all(f32[4,2,32,128]{3,2,1,0:T(8,128)S(1)} %broadcast_in_dim.25), channel_id=1, replica_groups={{0,128,256,384},{8,136,264,392},{16,144,272,400},{24,152,280,408},{32,1..., dimensions={0} | all-to-all | bytes 262144 | tf_op jit(solution)/shard_map/all_to_all | solution.py:284
  57.1 0.7 fusion.2
  57.8 12.0 %all-to-all-start.2 = ((f16[16,32,128]{2,1,0:T(8,128)(2,1)}), f16[16,32,128]{2,1,0:T(8,128)(2,1)S(1)}, u32[]{:S(2)}, u32[]{:S(2)}) async-start(f16[16,32,128]{2,1,0:T(8,128)(2,1)} %fusion.2), calls=%async_computation.2 | async-start | bytes 262144 | tf_op jit(solution)/shard_map/all_to_all | solution.py:289
  69.8 5.1 %collective-permute-start.6 = (f32[1]{0:T(128)}, f32[1]{0:T(128)}, u32[]{:S(2)}, u32[]{:S(2)}) collective-permute-start(f32[1]{0:T(128)} %bitcast.6), channel_id=1, source_target_pairs={{0,8},{8,16},{16,24},{24,32},{32,40},{40,48},{48,56},{56,64},{64,7... | collective-permute-start | bytes 20 | tf_op jit(solution)/shard_map/ppermute | solution.py:290
  74.9 3.8 %collective-permute-done.6 = f32[1]{0:T(128)} collective-permute-done((f32[1]{0:T(128)}, f32[1]{0:T(128)}, u32[]{:S(2)}, u32[]{:S(2)}) %collective-permute-start.6) | collective-permute-done | bytes 36 | tf_op jit(solution)/shard_map/ppermute | solution.py:290
  78.7 4.2 %all-to-all-done.2 = f16[16,32,128]{2,1,0:T(8,128)(2,1)S(1)} async-done(((f16[16,32,128]{2,1,0:T(8,128)(2,1)}), f16[16,32,128]{2,1,0:T(8,128)(2,1)S(1)}, u32[]{:S(2)}, u32[]{:S(2)}) %all-to-all-start.2) | async-done | bytes 131104 | tf_op jit(solution)/shard_map/all_to_all | solution.py:289
  82.9 0.9 %copy.13 = f32[1,32,16,128]{3,2,1,0:T(8,128)} copy(f32[1,32,16,128]{3,1,2,0:T(8,128)S(1)} %convert_bitcast_fusion) | data formatting | bytes 524288
  (11 shorter events, 0.1 us)
Async XLA Ops:
  2.4 20.8 %collective-permute-start = (bf16[17,32,128]{2,1,0:T(8,128)(2,1)S(1)}, bf16[17,32,128]{2,1,0:T(8,128)(2,1)S(1)}, u32[]{:S(2)}, u32[]{:S(2)}) collective-permute-start(bf16[17,32,128]{2,1,0:T(8,128)(2,1)S(1)} %get-tuple-element.25), channel_id=1, source_target_pairs={{8,0},{16,8},{24,16},{32,24},{40,32},{48,40},{56,48},{64,56},{72,6... | collective-permute-start | bytes 417800 | tf_op jit(solution)/shard_map/ppermute | solution.py:241
  16.0 4.7 %collective-permute-start.1 = (bf16[4,32,128]{2,1,0:T(8,128)(2,1)S(1)}, bf16[4,32,128]{2,1,0:T(8,128)(2,1)S(1)}, u32[]{:S(2)}, u32[]{:S(2)}) collective-permute-start(bf16[4,32,128]{2,1,0:T(8,128)(2,1)S(1)} %get-tuple-element.26), channel_id=1, source_target_pairs={{0,1},{1,0},{2,3},{3,2},{4,5},{5,4},{6,7},{7,6},{8,9},{9,8},{10,11... | collective-permute-start | bytes 98312 | tf_op jit(solution)/shard_map/ppermute | solution.py:243
  17.9 5.2 %collective-permute-start.2 = (bf16[4,32,128]{2,1,0:T(8,128)(2,1)S(1)}, bf16[4,32,128]{2,1,0:T(8,128)(2,1)S(1)}, u32[]{:S(2)}, u32[]{:S(2)}) collective-permute-start(bf16[4,32,128]{2,1,0:T(8,128)(2,1)S(1)} %get-tuple-element.27), channel_id=1, source_target_pairs={{1,2},{3,4},{5,6},{2,1},{4,3},{6,5},{9,10},{11,12},{13,14},{10,9},... | collective-permute-start | bytes 98312 | tf_op jit(solution)/shard_map/ppermute | solution.py:242
  25.9 20.8 %all-to-all-start = ((f16[16,2,32,128]{3,2,1,0:T(8,128)(2,1)}), f16[16,2,32,128]{3,2,1,0:T(8,128)(2,1)S(1)}, u32[]{:S(2)}, u32[]{:S(2)}) async-start(f16[16,2,32,128]{3,2,1,0:T(8,128)(2,1)} %convert_element_type.450), calls=%async_computation | async-start | bytes 524288 | tf_op jit(solution)/shard_map/all_to_all | solution.py:264
  30.0 3.1 %collective-permute-start.3 = (f32[1,128]{1,0:T(1,128)S(1)}, f32[1,128]{1,0:T(1,128)S(1)}, u32[]{:S(2)}, u32[]{:S(2)}) collective-permute-start(f32[1,128]{1,0:T(1,128)S(1)} %get-tuple-element.33), channel_id=1, source_target_pairs={{0,1},{1,0},{2,3},{3,2},{4,5},{5,4},{6,7},{7,6},{8,9},{9,8},{10,11... | collective-permute-start | bytes 1544 | tf_op jit(solution)/shard_map/ppermute | solution.py:266
  33.1 5.5 %collective-permute-start.4 = (f32[1,128]{1,0:T(1,128)S(1)}, f32[1,128]{1,0:T(1,128)S(1)}, u32[]{:S(2)}, u32[]{:S(2)}) collective-permute-start(f32[1,128]{1,0:T(1,128)S(1)} %add.178), channel_id=1, source_target_pairs={{0,2},{1,3},{2,0},{3,1},{4,6},{5,7},{6,4},{7,5},{8,10},{9,11},{10,... | collective-permute-start | bytes 1544 | tf_op jit(solution)/shard_map/ppermute | solution.py:266
  38.5 7.0 %collective-permute-start.5 = (f32[1,128]{1,0:T(1,128)S(1)}, f32[1,128]{1,0:T(1,128)S(1)}, u32[]{:S(2)}, u32[]{:S(2)}) collective-permute-start(f32[1,128]{1,0:T(1,128)S(1)} %add.179), channel_id=1, source_target_pairs={{0,4},{1,5},{2,6},{3,7},{4,0},{5,1},{6,2},{7,3},{8,12},{9,13},{10,... | collective-permute-start | bytes 1544 | tf_op jit(solution)/shard_map/ppermute | solution.py:266
  57.8 25.1 %all-to-all-start.2 = ((f16[16,32,128]{2,1,0:T(8,128)(2,1)}), f16[16,32,128]{2,1,0:T(8,128)(2,1)S(1)}, u32[]{:S(2)}, u32[]{:S(2)}) async-start(f16[16,32,128]{2,1,0:T(8,128)(2,1)} %fusion.2), calls=%async_computation.2 | async-start | bytes 262144 | tf_op jit(solution)/shard_map/all_to_all | solution.py:289
  69.8 8.9 %collective-permute-start.6 = (f32[1]{0:T(128)}, f32[1]{0:T(128)}, u32[]{:S(2)}, u32[]{:S(2)}) collective-permute-start(f32[1]{0:T(128)} %bitcast.6), channel_id=1, source_target_pairs={{0,8},{8,16},{16,24},{24,32},{32,40},{40,48},{48,56},{56,64},{64,7... | collective-permute-start | bytes 20 | tf_op jit(solution)/shard_map/ppermute | solution.py:290

commit v5 on v4

--- a/solution.py
+++ b/solution.py
@@ -21,7 +21,7 @@
 
 
 def groups_of(rows):
-    return [(g, min(GROUP, rows - g)) for g in range(0, rows, GROUP)]
+    return [(g, min(GROUP, (rows - g) // 2)) for g in range(0, rows, 2 * GROUP)]
 
 
 def rounded(value):
@@ -135,8 +135,8 @@
 
     def product(band, outs, src, g, n):
         k = (n + 2) * 128
-        rhs = src[g : g + n + 2].reshape(k, width)
-        return jnp.dot(band[: n * outs, :k], rhs, preferred_element_type=jnp.float32)
+        sides = [src[at : at + n + 2].reshape(k, width) for at in (g, g + n)]
+        return jnp.dot(band[: n * outs, :k], jnp.concatenate(sides, axis=1), preferred_element_type=jnp.float32)
 
     top = strip == 0
     bottom = strip == lax.axis_size("space") - 1
@@ -147,9 +147,10 @@
                 band_ref[r * chans : (r + 1) * chans, (r + a) * 128 : (r + a + 1) * 128] = wh_ref[layer, a]
         halo = HALO - 1 - layer
         for g, n in groups_of(rows + 2 * halo):
-            acc = product(band_ref, chans, src, g, n).reshape(n, chans, width)
-            for j in range(n):
-                pre = acc[j] + biases[layer]
+            acc = product(band_ref, chans, src, g, n).reshape(n, chans, 2 * width)
+            for j in range(2 * n):
+                side = j // n
+                pre = acc[j % n, :, side * width : (side + 1) * width] + biases[layer]
                 value = 0.5 * pre * (1.0 + jnp.tanh(0.5 * pre))
                 if g + j < halo:
                     value = jnp.where(top, 0.0, value)
@@ -163,12 +164,13 @@
             head_ref[r * 2 * chans : (r + 1) * 2 * chans, (r + a) * 128 : (r + a + 1) * 128] = wo_ref[a]
     total = jnp.zeros((chans, width), jnp.float32)
     for g, n in groups_of(rows):
-        acc = product(head_ref, 2 * chans, src, g, n).reshape(n, 2 * chans, width)
-        for j in range(n):
-            row = g + j
+        acc = product(head_ref, 2 * chans, src, g, n).reshape(n, 2 * chans, 2 * width)
+        for j in range(2 * n):
+            row, side = g + j, j // n
+            both = acc[j % n, :, side * width : (side + 1) * width]
             guess = guess_ref[row]
-            cand = jnp.tanh(acc[j, :chans] + cand_bias + skip * guess)
-            rest = 1.0 / (1.0 + jnp.exp(acc[j, chans:] + gate_bias))
+            cand = jnp.tanh(both[:chans] + cand_bias + skip * guess)
+            rest = 1.0 / (1.0 + jnp.exp(both[chans:] + gate_bias))
             slope = (1.0 - cand * cand) * skip
             maps_ref[row, 0] = rest * (1.0 - slope)
             maps_ref[row, 1] = rest * (cand - slope * guess)
@@ -262,11 +264,10 @@
     z_groups = [[x * NZ + z for z in range(NZ)] for x in range(NX)]
     x_groups = [[x * NZ + z for x in range(NX)] for z in range(NZ)]
     sent = lax.all_to_all(maps.astype(jnp.float16), "tm", 0, 0, axis_index_groups=z_groups)
-    for bit in (1, 2, 4):
+    for bit in (1, 2, 6):
         partial = partial + lax.ppermute(partial, "space", [(s, s ^ bit) for s in range(n_space)])
-    res_msq = jnp.sum(partial).reshape(1) / (chans * rows * width * n_space)
     flags = [mine == NX - 1] + [x < mine for x in range(NX - 1)]
-    sent, res_msq, flags = lax.optimization_barrier((sent, res_msq, flags))
+    sent, partial, flags = lax.optimization_barrier((sent, partial, flags))
 
     steps = [(1.0 - sent[z, 0].astype(f32), sent[z, 1].astype(f32)) for z in range(NZ)]
     block_a, block_b = steps[0]
@@ -287,7 +288,8 @@
         state = jnp.where(flags[x + 1], blocks[x, 0] * state + blocks[x, 1], state)
     states = (pref[:, 0] * state + pref[:, 1]).astype(jnp.float16)
     back = lax.all_to_all(states, "tm", 0, 0, axis_index_groups=z_groups)
-    res_msq = lax.ppermute(res_msq, "tm", [(t, (t + 1) % n_tm) for t in range(n_tm)])
+    partial = lax.ppermute(partial, "tm", [(t, (t + 1) % n_tm) for t in range(n_tm)])
+    res_msq = jnp.sum(partial).reshape(1) / (chans * rows * width * n_space)
     back, res_msq = lax.optimization_barrier((back, res_msq))
     new_traj = jnp.swapaxes(back.astype(f32), 0, 1)[None]
     return new_traj, res_msq

time: 86.1 us -> 83.8 us (0.973)
  starting transfers between devices: 47.1 us -> 44.3 us
  waiting for transfers between devices: 18.2 us -> 19.5 us
    ppermute x1, starting transfers between devices: 5.11 us -> 3.82 us  [body(): lax.ppermute(partial, 'tm', [(t, (t + 1) % n_tm) for t in range(n_tm)])]
    ppermute x1, waiting for transfers between devices: 3.78 us -> 4.95 us  [body(): lax.ppermute(partial, 'tm', [(t, (t + 1) % n_tm) for t in range(n_tm)])]
    all_to_all x1, waiting for transfers between devices: 4.21 us -> 3.07 us  [body(): back = lax.all_to_all(states, 'tm', 0, 0, axis_index_groups=z_groups)]
    ppermute x3, starting transfers between devices: 7.67 us -> 6.56 us  [body(): lax.ppermute(partial, 'space', [(s, s ^ bit) for s in range(n_space)])]
  transfers between devices with their start and end apart: 9 -> 9, of which waited for: 6 -> 7; matrix products, arithmetic and copies ran while one was open for 1% -> 1% of each run, Pallas kernels for 0% -> 0%
where the time goes in v5:
time: 83.8 us; the launch traced here: 83.3 us
  starting transfers between devices  44.3 us (53%)
  waiting for transfers between devices  19.5 us (23%)
  blocking collectives  10.1 us (12%)
  Pallas kernels  3.7 us (4%)
  between operations  2.6 us (3%)
  other arithmetic  2.26 us (3%)
  local copies, waits for them, and re-layouts  0.87 us (1%)
    ppermute x1, starting transfers between devices, body(): lax.ppermute(shift, 'tm', [((t + 1) % n_tm, t) for t in range(n_tm)])  13.6 us
    all_to_all x1, starting transfers between devices, body(): back = lax.all_to_all(states, 'tm', 0, 0, axis_index_groups=z_groups)  11.6 us
    all_to_all x1, blocking collectives, body(): blocks = lax.all_to_all(copies, 'tm', 0, 0, axis_index_groups=x_groups)  10.1 us
    ppermute x3, waiting for transfers between devices, body(): lax.ppermute(partial, 'space', [(s, s ^ bit) for s in range(n_space)])  8.55 us
    ppermute x3, starting transfers between devices, body(): lax.ppermute(partial, 'space', [(s, s ^ bit) for s in range(n_space)])  6.56 us
    ppermute x1, waiting for transfers between devices, body(): lax.ppermute(partial, 'tm', [(t, (t + 1) % n_tm) for t in range(n_tm)])  4.95 us
    all_to_all x1, starting transfers between devices, body(): lax.all_to_all(maps.astype(jnp.float16), 'tm', 0, 0, axis_index_groups=z_...  4.06 us
    ppermute x1, starting transfers between devices, body(): lax.ppermute(partial, 'tm', [(t, (t + 1) % n_tm) for t in range(n_tm)])  3.82 us
  transfers between devices with their start and end apart: 9, of which 7 were waited for; matrix products, arithmetic and copies ran while one was open for 1% of the time, Pallas kernels for 0%

profile of v5, /device:TPU:24, one launch (start us, length us, event | category | flops | bytes accessed | tf_op | source)
XLA Modules:
  0.0 83.3 jit_solution(17530143752366228635)
XLA Ops:
  0.6 1.7 %sends.1 = (bf16[17,32,128]{2,1,0:T(8,128)(2,1)S(1)}, bf16[4,32,128]{2,1,0:T(8,128)(2,1)S(1)}, bf16[4,32,128]{2,1,0:T(8,128)(2,1)S(1)}, f32[16,32,128]{2,1,0:T(8...) custom-call(f32[512,128]{1,0:T(8,128)} %bitcast.159, ...), custom_call_target="tpu_custom_call" | custom-call | tf_op jit(solution)/shard_map/sends/pallas_call | solution.py:212
  2.4 13.6 %collective-permute-start = (bf16[17,32,128]{2,1,0:T(8,128)(2,1)S(1)}, bf16[17,32,128]{2,1,0:T(8,128)(2,1)S(1)}, u32[]{:S(2)}, u32[]{:S(2)}) collective-permute-start(bf16[17,32,128]{2,1,0:T(8,128)(2,1)S(1)} %get-tuple-element.25), channel_id=1, source_target_pairs={{8,0},{16,8},{24,16},{32,24},{40,32},{48,40},{56,48},{64,56},{72,6... | collective-permute-start | bytes 417800 | tf_op jit(solution)/shard_map/ppermute | solution.py:243
  16.0 1.9 %collective-permute-start.1 = (bf16[4,32,128]{2,1,0:T(8,128)(2,1)S(1)}, bf16[4,32,128]{2,1,0:T(8,128)(2,1)S(1)}, u32[]{:S(2)}, u32[]{:S(2)}) collective-permute-start(bf16[4,32,128]{2,1,0:T(8,128)(2,1)S(1)} %get-tuple-element.26), channel_id=1, source_target_pairs={{0,1},{1,0},{2,3},{3,2},{4,5},{5,4},{6,7},{7,6},{8,9},{9,8},{10,11... | collective-permute-start | bytes 98312 | tf_op jit(solution)/shard_map/ppermute | solution.py:245
  17.9 2.8 %collective-permute-start.2 = (bf16[4,32,128]{2,1,0:T(8,128)(2,1)S(1)}, bf16[4,32,128]{2,1,0:T(8,128)(2,1)S(1)}, u32[]{:S(2)}, u32[]{:S(2)}) collective-permute-start(bf16[4,32,128]{2,1,0:T(8,128)(2,1)S(1)} %get-tuple-element.27), channel_id=1, source_target_pairs={{1,2},{3,4},{5,6},{2,1},{4,3},{6,5},{9,10},{11,12},{13,14},{10,9},... | collective-permute-start | bytes 98312 | tf_op jit(solution)/shard_map/ppermute | solution.py:244
  20.7 2.5 %collective-permute-done.2.chip_ref = bf16[4,32,128]{2,1,0:T(8,128)(2,1)S(1)} collective-permute-done((bf16[4,32,128]{2,1,0:T(8,128)(2,1)S(1)}, bf16[4,32,128]{2,1,0:T(8,128)(2,1)S(1)}, u32[]{:S(2)}, u32[]{:S(2)}) %collective-permute-start.2) | collective-permute-done | bytes 32800 | tf_op jit(solution)/shard_map/ppermute | solution.py:244
  23.1 2.0 %dynamics.1 = (f32[16,2,32,128]{3,2,1,0:T(8,128)S(1)}, f32[1,128]{1,0:T(1,128)S(1)}) custom-call(f32[16,32,128]{2,1,0:T(8,128)S(1)} %get-tuple-element.24.guess_ref, bf16[17,32,128]{2,1,0:T(8,128)(2,1)S(1)} %collective-permute-done.shift_ref, bf16[4,32,128]{2,1,0:T(8,128)(2,1)S(1)} %collective-permute-done.1.pair_ref, ...), custom_call_target="tpu_custom_call" | custom-call | tf_op jit(solution)/shard_map/dynamics/pallas_call | solution.py:248
  25.1 0.8 convert_element_type.450
  25.8 4.1 %all-to-all-start = ((f16[16,2,32,128]{3,2,1,0:T(8,128)(2,1)}), f16[16,2,32,128]{3,2,1,0:T(8,128)(2,1)S(1)}, u32[]{:S(2)}, u32[]{:S(2)}) async-start(f16[16,2,32,128]{3,2,1,0:T(8,128)(2,1)} %convert_element_type.450), calls=%async_computation | async-start | bytes 524288 | tf_op jit(solution)/shard_map/all_to_all | solution.py:266
  29.9 1.9 %collective-permute-start.3 = (f32[1,128]{1,0:T(1,128)S(1)}, f32[1,128]{1,0:T(1,128)S(1)}, u32[]{:S(2)}, u32[]{:S(2)}) collective-permute-start(f32[1,128]{1,0:T(1,128)S(1)} %get-tuple-element.33), channel_id=1, source_target_pairs={{0,1},{1,0},{2,3},{3,2},{4,5},{5,4},{6,7},{7,6},{8,9},{9,8},{10,11... | collective-permute-start | bytes 1544 | tf_op jit(solution)/shard_map/ppermute | solution.py:268
  31.8 1.1 %collective-permute-done.3 = f32[1,128]{1,0:T(1,128)S(1)} collective-permute-done((f32[1,128]{1,0:T(1,128)S(1)}, f32[1,128]{1,0:T(1,128)S(1)}, u32[]{:S(2)}, u32[]{:S(2)}) %collective-permute-start.3) | collective-permute-done | bytes 544 | tf_op jit(solution)/shard_map/ppermute | solution.py:268
  33.0 2.6 %collective-permute-start.4 = (f32[1,128]{1,0:T(1,128)S(1)}, f32[1,128]{1,0:T(1,128)S(1)}, u32[]{:S(2)}, u32[]{:S(2)}) collective-permute-start(f32[1,128]{1,0:T(1,128)S(1)} %add.178), channel_id=1, source_target_pairs={{0,2},{1,3},{2,0},{3,1},{4,6},{5,7},{6,4},{7,5},{8,10},{9,11},{10,... | collective-permute-start | bytes 1544 | tf_op jit(solution)/shard_map/ppermute | solution.py:268
  35.6 2.8 %collective-permute-done.4 = f32[1,128]{1,0:T(1,128)S(1)} collective-permute-done((f32[1,128]{1,0:T(1,128)S(1)}, f32[1,128]{1,0:T(1,128)S(1)}, u32[]{:S(2)}, u32[]{:S(2)}) %collective-permute-start.4) | collective-permute-done | bytes 544 | tf_op jit(solution)/shard_map/ppermute | solution.py:268
  38.4 2.0 %collective-permute-start.5 = (f32[1,128]{1,0:T(1,128)S(1)}, f32[1,128]{1,0:T(1,128)S(1)}, u32[]{:S(2)}, u32[]{:S(2)}) collective-permute-start(f32[1,128]{1,0:T(1,128)S(1)} %add.179), channel_id=1, source_target_pairs={{0,6},{1,7},{2,4},{3,5},{4,2},{5,3},{6,0},{7,1},{8,14},{9,15},{10,... | collective-permute-start | bytes 1544 | tf_op jit(solution)/shard_map/ppermute | solution.py:268
  40.5 4.6 %collective-permute-done.5 = f32[1,128]{1,0:T(1,128)S(1)} collective-permute-done((f32[1,128]{1,0:T(1,128)S(1)}, f32[1,128]{1,0:T(1,128)S(1)}, u32[]{:S(2)}, u32[]{:S(2)}) %collective-permute-start.5) | collective-permute-done | bytes 544 | tf_op jit(solution)/shard_map/ppermute | solution.py:268
  45.1 0.5 all-to-all-done
  45.6 0.1 add_select_fusion
  45.8 10.1 %all_to_all.15 = f32[4,2,32,128]{3,2,1,0:T(8,128)S(1)} all-to-all(f32[4,2,32,128]{3,2,1,0:T(8,128)S(1)} %broadcast_in_dim.25), channel_id=1, replica_groups={{0,128,256,384},{8,136,264,392},{16,144,272,400},{24,152,280,408},{32,1..., dimensions={0} | all-to-all | bytes 262144 | tf_op jit(solution)/shard_map/all_to_all | solution.py:285
  55.9 0.7 fusion.2
  56.6 11.6 %all-to-all-start.2 = ((f16[16,32,128]{2,1,0:T(8,128)(2,1)}), f16[16,32,128]{2,1,0:T(8,128)(2,1)S(1)}, u32[]{:S(2)}, u32[]{:S(2)}) async-start(f16[16,32,128]{2,1,0:T(8,128)(2,1)} %fusion.2), calls=%async_computation.2 | async-start | bytes 262144 | tf_op jit(solution)/shard_map/all_to_all | solution.py:290
  68.1 3.8 %collective-permute-start.6 = (f32[1,128]{1,0:T(1,128)S(1)}, f32[1,128]{1,0:T(1,128)S(1)}, u32[]{:S(2)}, u32[]{:S(2)}) collective-permute-start(f32[1,128]{1,0:T(1,128)S(1)} %add.180), channel_id=1, source_target_pairs={{0,8},{8,16},{16,24},{24,32},{32,40},{40,48},{48,56},{56,64},{64,7... | collective-permute-start | bytes 1544 | tf_op jit(solution)/shard_map/ppermute | solution.py:291
  72.0 5.0 %collective-permute-done.6 = f32[1,128]{1,0:T(1,128)S(1)} collective-permute-done((f32[1,128]{1,0:T(1,128)S(1)}, f32[1,128]{1,0:T(1,128)S(1)}, u32[]{:S(2)}, u32[]{:S(2)}) %collective-permute-start.6) | collective-permute-done | bytes 544 | tf_op jit(solution)/shard_map/ppermute | solution.py:291
  76.9 0.6 reduce_sum.9
  78.2 3.1 %all-to-all-done.2 = f16[16,32,128]{2,1,0:T(8,128)(2,1)S(1)} async-done(((f16[16,32,128]{2,1,0:T(8,128)(2,1)}), f16[16,32,128]{2,1,0:T(8,128)(2,1)S(1)}, u32[]{:S(2)}, u32[]{:S(2)}) %all-to-all-start.2) | async-done | bytes 131104 | tf_op jit(solution)/shard_map/all_to_all | solution.py:290
  81.3 0.9 %copy.13 = f32[1,32,16,128]{3,2,1,0:T(8,128)} copy(f32[1,32,16,128]{3,1,2,0:T(8,128)S(1)} %convert_bitcast_fusion) | data formatting | bytes 524288
  (12 shorter events, 0.2 us)
Async XLA Ops:
  2.4 20.8 %collective-permute-start = (bf16[17,32,128]{2,1,0:T(8,128)(2,1)S(1)}, bf16[17,32,128]{2,1,0:T(8,128)(2,1)S(1)}, u32[]{:S(2)}, u32[]{:S(2)}) collective-permute-start(bf16[17,32,128]{2,1,0:T(8,128)(2,1)S(1)} %get-tuple-element.25), channel_id=1, source_target_pairs={{8,0},{16,8},{24,16},{32,24},{40,32},{48,40},{56,48},{64,56},{72,6... | collective-permute-start | bytes 417800 | tf_op jit(solution)/shard_map/ppermute | solution.py:243
  16.0 4.7 %collective-permute-start.1 = (bf16[4,32,128]{2,1,0:T(8,128)(2,1)S(1)}, bf16[4,32,128]{2,1,0:T(8,128)(2,1)S(1)}, u32[]{:S(2)}, u32[]{:S(2)}) collective-permute-start(bf16[4,32,128]{2,1,0:T(8,128)(2,1)S(1)} %get-tuple-element.26), channel_id=1, source_target_pairs={{0,1},{1,0},{2,3},{3,2},{4,5},{5,4},{6,7},{7,6},{8,9},{9,8},{10,11... | collective-permute-start | bytes 98312 | tf_op jit(solution)/shard_map/ppermute | solution.py:245
  17.9 5.2 %collective-permute-start.2 = (bf16[4,32,128]{2,1,0:T(8,128)(2,1)S(1)}, bf16[4,32,128]{2,1,0:T(8,128)(2,1)S(1)}, u32[]{:S(2)}, u32[]{:S(2)}) collective-permute-start(bf16[4,32,128]{2,1,0:T(8,128)(2,1)S(1)} %get-tuple-element.27), channel_id=1, source_target_pairs={{1,2},{3,4},{5,6},{2,1},{4,3},{6,5},{9,10},{11,12},{13,14},{10,9},... | collective-permute-start | bytes 98312 | tf_op jit(solution)/shard_map/ppermute | solution.py:244
  25.8 19.7 %all-to-all-start = ((f16[16,2,32,128]{3,2,1,0:T(8,128)(2,1)}), f16[16,2,32,128]{3,2,1,0:T(8,128)(2,1)S(1)}, u32[]{:S(2)}, u32[]{:S(2)}) async-start(f16[16,2,32,128]{3,2,1,0:T(8,128)(2,1)} %convert_element_type.450), calls=%async_computation | async-start | bytes 524288 | tf_op jit(solution)/shard_map/all_to_all | solution.py:266
  29.9 3.1 %collective-permute-start.3 = (f32[1,128]{1,0:T(1,128)S(1)}, f32[1,128]{1,0:T(1,128)S(1)}, u32[]{:S(2)}, u32[]{:S(2)}) collective-permute-start(f32[1,128]{1,0:T(1,128)S(1)} %get-tuple-element.33), channel_id=1, source_target_pairs={{0,1},{1,0},{2,3},{3,2},{4,5},{5,4},{6,7},{7,6},{8,9},{9,8},{10,11... | collective-permute-start | bytes 1544 | tf_op jit(solution)/shard_map/ppermute | solution.py:268
  33.0 5.5 %collective-permute-start.4 = (f32[1,128]{1,0:T(1,128)S(1)}, f32[1,128]{1,0:T(1,128)S(1)}, u32[]{:S(2)}, u32[]{:S(2)}) collective-permute-start(f32[1,128]{1,0:T(1,128)S(1)} %add.178), channel_id=1, source_target_pairs={{0,2},{1,3},{2,0},{3,1},{4,6},{5,7},{6,4},{7,5},{8,10},{9,11},{10,... | collective-permute-start | bytes 1544 | tf_op jit(solution)/shard_map/ppermute | solution.py:268
  38.4 6.7 %collective-permute-start.5 = (f32[1,128]{1,0:T(1,128)S(1)}, f32[1,128]{1,0:T(1,128)S(1)}, u32[]{:S(2)}, u32[]{:S(2)}) collective-permute-start(f32[1,128]{1,0:T(1,128)S(1)} %add.179), channel_id=1, source_target_pairs={{0,6},{1,7},{2,4},{3,5},{4,2},{5,3},{6,0},{7,1},{8,14},{9,15},{10,... | collective-permute-start | bytes 1544 | tf_op jit(solution)/shard_map/ppermute | solution.py:268
  56.6 24.7 %all-to-all-start.2 = ((f16[16,32,128]{2,1,0:T(8,128)(2,1)}), f16[16,32,128]{2,1,0:T(8,128)(2,1)S(1)}, u32[]{:S(2)}, u32[]{:S(2)}) async-start(f16[16,32,128]{2,1,0:T(8,128)(2,1)} %fusion.2), calls=%async_computation.2 | async-start | bytes 262144 | tf_op jit(solution)/shard_map/all_to_all | solution.py:290
  68.1 8.8 %collective-permute-start.6 = (f32[1,128]{1,0:T(1,128)S(1)}, f32[1,128]{1,0:T(1,128)S(1)}, u32[]{:S(2)}, u32[]{:S(2)}) collective-permute-start(f32[1,128]{1,0:T(1,128)S(1)} %add.180), channel_id=1, source_target_pairs={{0,8},{8,16},{16,24},{24,32},{32,40},{40,48},{48,56},{56,64},{64,7... | collective-permute-start | bytes 1544 | tf_op jit(solution)/shard_map/ppermute | solution.py:291

commit v6 on v5

--- a/solution.py
+++ b/solution.py
@@ -30,10 +30,11 @@
 
 def send_kernel(
     traj_hbm, start_hbm, act_hbm, hb_hbm, cb_hbm, gb_hbm, sk_hbm, proj_hbm, wh_hbm, wo_hbm,
-    shift_ref, pair_ref, chip_ref, guess_ref, begin_ref, cols_ref, proj_ref, th_ref, to_ref,
-    traj_ref, start_ref, act_ref, hb_ref, cb_ref, gb_ref, sk_ref, wh_ref, wo_ref, line_ref, sems,
+    shift_ref, pair_ref, chip_ref, traj_ref, start_ref, hb_ref, cb_ref, gb_ref, sk_ref, proj_ref, wh_ref, wo_ref,
+    act_ref, line_ref, sems,
 ):
-    rows, chans, width = guess_ref.shape
+    chans, _ = shift_ref.shape[1:]
+    rows = shift_ref.shape[0] - 1
     moves = [
         pltpu.make_async_copy(source, target, sems.at[i])
         for i, (source, target) in enumerate(
@@ -64,6 +65,24 @@
         line_ref[part : part + 1, : piece.shape[1]] = piece
         rest = rest - piece
     shift_ref[rows] = line_ref[...].astype(jnp.bfloat16)
+    for r in range(rows):
+        shift_ref[r] = traj_ref[pl.ds(r, chans, stride=rows), :].astype(jnp.bfloat16)
+
+    def guess(r):
+        return jnp.where(last, start_ref[pl.ds(r, chans, stride=rows), :].astype(jnp.bfloat16), shift_ref[r])
+
+    for r in range(HALO):
+        upper, lower = guess(r), guess(rows - HALO + r)
+        pair_ref[r] = jnp.where(even, lower, upper)
+        chip_ref[r] = jnp.where(even, upper, lower)
+
+
+def prep_kernel(
+    traj_ref, start_ref, hb_ref, cb_ref, gb_ref, sk_ref, wh_ref, wo_ref,
+    guess_ref, begin_ref, cols_ref, th_ref, to_ref,
+):
+    rows, chans, width = guess_ref.shape
+    last = lax.axis_index("tm") == lax.axis_size("tm") - 1
 
     def spread(vec):
         return jnp.broadcast_to(column(vec), (chans, width))
@@ -75,15 +94,9 @@
     cols_ref[5] = spread(sk_ref[...])
     for r in range(rows):
         at = pl.ds(r, chans, stride=rows)
-        mine = traj_ref[at, :]
-        shift_ref[r] = mine.astype(jnp.bfloat16)
-        guess_ref[r] = jnp.where(last, start_ref[at, :], mine)
+        guess_ref[r] = jnp.where(last, start_ref[at, :], traj_ref[at, :])
     place = lax.rem(lax.axis_index("tm"), NZ)
     begin_ref[...] = start_ref[pl.ds(place, chans, stride=rows), :]
-    for r in range(HALO):
-        upper, lower = guess_ref[r], guess_ref[rows - HALO + r]
-        pair_ref[r] = jnp.where(even, lower, upper).astype(jnp.bfloat16)
-        chip_ref[r] = jnp.where(even, upper, lower).astype(jnp.bfloat16)
     for a in range(3):
         for layer in range(3):
             th_ref[layer, a] = tile_of([wh_ref[layer, 3 * a + b].astype(jnp.float32) for b in range(3)])
@@ -209,36 +222,46 @@
     loaded = (
         flat, begin, actions, hidden_b, cand_b[None], gate_b[None], skip[None], act_proj, hidden_w, jnp.swapaxes(head_w, 1, 2),
     )
-    shift, pair, chip, guess, entry, cols, proj, taps, head_taps = pl.pallas_call(
+    one = jax.ShapeDtypeStruct((1, chans), f32)
+    shift, pair, chip, *kept = pl.pallas_call(
         send_kernel,
         in_specs=[pl.BlockSpec(memory_space=pltpu.HBM)] * len(loaded),
         out_shape=(
             jax.ShapeDtypeStruct((rows + 1, chans, width), bf16),
             jax.ShapeDtypeStruct((HALO, chans, width), bf16),
             jax.ShapeDtypeStruct((HALO, chans, width), bf16),
-            jax.ShapeDtypeStruct((rows, chans, width), f32),
-            jax.ShapeDtypeStruct((chans, width), f32),
-            jax.ShapeDtypeStruct((6, chans, width), f32),
+            jax.ShapeDtypeStruct((chans * rows, width), f32),
+            jax.ShapeDtypeStruct((chans * rows, width), f32),
+            jax.ShapeDtypeStruct(hidden_b.shape, f32),
+            one,
+            one,
+            one,
             jax.ShapeDtypeStruct(act_proj.shape, f32),
-            jax.ShapeDtypeStruct((3, 3, chans, 128), bf16),
-            jax.ShapeDtypeStruct((3, 2 * chans, 128), bf16),
+            jax.ShapeDtypeStruct(hidden_w.shape, bf16),
+            jax.ShapeDtypeStruct((9, chans, 2 * chans), bf16),
         ),
         scratch_shapes=[
-            pltpu.VMEM((chans * rows, width), f32),
-            pltpu.VMEM((chans * rows, width), f32),
             pltpu.VMEM(actions.shape, f32),
-            pltpu.VMEM(hidden_b.shape, f32),
-            pltpu.VMEM((1, chans), f32),
-            pltpu.VMEM((1, chans), f32),
-            pltpu.VMEM((1, chans), f32),
-            pltpu.VMEM(hidden_w.shape, bf16),
-            pltpu.VMEM((9, chans, 2 * chans), bf16),
             pltpu.VMEM((chans, width), f32),
             pltpu.SemaphoreType.DMA((len(loaded),)),
         ],
         compiler_params=params(),
         name="sends",
     )(*[pltpu.with_memory_space_constraint(value, pltpu.HBM) for value in loaded])
+    proj = kept.pop(6)
+    guess, entry, cols, taps, head_taps = pl.pallas_call(
+        prep_kernel,
+        out_shape=(
+            jax.ShapeDtypeStruct((rows, chans, width), f32),
+            jax.ShapeDtypeStruct((chans, width), f32),
+            jax.ShapeDtypeStruct((6, chans, width), f32),
+            jax.ShapeDtypeStruct((3, 3, chans, 128), bf16),
+            jax.ShapeDtypeStruct((3, 2 * chans, 128), bf16),
+        ),
+        compiler_params=params(),
+        cost_estimate=pl.CostEstimate(flops=2**20, bytes_accessed=2**20, transcendentals=0),
+        name="prep",
+    )(*kept)
     crossing = [(s, s + 1) for s in range(1, n_space - 1, 2)]
     shift = lax.ppermute(shift, "tm", [((t + 1) % n_tm, t) for t in range(n_tm)])
     chip = lax.ppermute(chip, "space", crossing + [(b, a) for a, b in crossing])
@@ -281,8 +304,8 @@
         cost_estimate=pl.CostEstimate(flops=2**20, bytes_accessed=2**20, transcendentals=0),
         name="prefix",
     )(sent.astype(f32))
-    copies, pref, entry = lax.optimization_barrier((jnp.broadcast_to(block[None], (NX,) + block.shape), pref, entry))
-    blocks = lax.all_to_all(copies, "tm", 0, 0, axis_index_groups=x_groups)
+    copies, pref, entry = lax.optimization_barrier((jnp.broadcast_to(block.astype(jnp.float16)[None], (NX,) + block.shape), pref, entry))
+    blocks = lax.all_to_all(copies, "tm", 0, 0, axis_index_groups=x_groups).astype(f32)
     state = blocks[NX - 1, 0] * entry + blocks[NX - 1, 1]
     for x in range(NX - 1):
         state = jnp.where(flags[x + 1], blocks[x, 0] * state + blocks[x, 1], state)

time: 83.8 us -> 83.2 us (level)
  no operation moved by 1% of the time
where the time goes in v6:
time: 83.2 us; the launch traced here: 82.7 us
  starting transfers between devices  44.3 us (53%)
  waiting for transfers between devices  19.1 us (23%)
  blocking collectives  9.72 us (12%)
  Pallas kernels  3.75 us (5%)
  between operations  2.61 us (3%)
  other arithmetic  2.28 us (3%)
  local copies, waits for them, and re-layouts  0.87 us (1%)
    ppermute x1, starting transfers between devices, body(): lax.ppermute(shift, 'tm', [((t + 1) % n_tm, t) for t in range(n_tm)])  13.6 us
    all_to_all x1, starting transfers between devices, body(): back = lax.all_to_all(states, 'tm', 0, 0, axis_index_groups=z_groups)  11.6 us
    all_to_all x1, blocking collectives, body(): lax.all_to_all(copies, 'tm', 0, 0, axis_index_groups=x_groups).astype(f32)  9.72 us
    ppermute x3, waiting for transfers between devices, body(): lax.ppermute(partial, 'space', [(s, s ^ bit) for s in range(n_space)])  8.55 us
    ppermute x3, starting transfers between devices, body(): lax.ppermute(partial, 'space', [(s, s ^ bit) for s in range(n_space)])  6.56 us
    ppermute x1, waiting for transfers between devices, body(): lax.ppermute(partial, 'tm', [(t, (t + 1) % n_tm) for t in range(n_tm)])  4.95 us
    all_to_all x1, starting transfers between devices, body(): lax.all_to_all(maps.astype(jnp.float16), 'tm', 0, 0, axis_index_groups=z_...  4.07 us
    ppermute x1, starting transfers between devices, body(): lax.ppermute(partial, 'tm', [(t, (t + 1) % n_tm) for t in range(n_tm)])  3.82 us
  transfers between devices with their start and end apart: 9, of which 7 were waited for; matrix products, arithmetic and copies ran while one was open for 1% of the time, Pallas kernels for 0%

profile of v6, /device:TPU:24, one launch (start us, length us, event | category | flops | bytes accessed | tf_op | source)
XLA Modules:
  0.0 82.7 jit_solution(3669052600787113733)
XLA Ops:
  0.6 1.4 %sends.1 = (bf16[17,32,128]{2,1,0:T(8,128)(2,1)S(1)}, bf16[4,32,128]{2,1,0:T(8,128)(2,1)S(1)}, bf16[4,32,128]{2,1,0:T(8,128)(2,1)S(1)}, f32[512,128]{1,0:T(8,128...) custom-call(f32[512,128]{1,0:T(8,128)} %bitcast.95, ...), custom_call_target="tpu_custom_call" | custom-call | tf_op jit(solution)/shard_map/sends/pallas_call | solution.py:226
  2.1 13.6 %collective-permute-start = (bf16[17,32,128]{2,1,0:T(8,128)(2,1)S(1)}, bf16[17,32,128]{2,1,0:T(8,128)(2,1)S(1)}, u32[]{:S(2)}, u32[]{:S(2)}) collective-permute-start(bf16[17,32,128]{2,1,0:T(8,128)(2,1)S(1)} %get-tuple-element.41), channel_id=1, source_target_pairs={{8,0},{16,8},{24,16},{32,24},{40,32},{48,40},{56,48},{64,56},{72,6... | collective-permute-start | bytes 417800 | tf_op jit(solution)/shard_map/ppermute | solution.py:266
  15.7 1.9 %collective-permute-start.1 = (bf16[4,32,128]{2,1,0:T(8,128)(2,1)S(1)}, bf16[4,32,128]{2,1,0:T(8,128)(2,1)S(1)}, u32[]{:S(2)}, u32[]{:S(2)}) collective-permute-start(bf16[4,32,128]{2,1,0:T(8,128)(2,1)S(1)} %get-tuple-element.42), channel_id=1, source_target_pairs={{0,1},{1,0},{2,3},{3,2},{4,5},{5,4},{6,7},{7,6},{8,9},{9,8},{10,11... | collective-permute-start | bytes 98312 | tf_op jit(solution)/shard_map/ppermute | solution.py:268
  17.6 2.8 %collective-permute-start.2 = (bf16[4,32,128]{2,1,0:T(8,128)(2,1)S(1)}, bf16[4,32,128]{2,1,0:T(8,128)(2,1)S(1)}, u32[]{:S(2)}, u32[]{:S(2)}) collective-permute-start(bf16[4,32,128]{2,1,0:T(8,128)(2,1)S(1)} %get-tuple-element.43), channel_id=1, source_target_pairs={{1,2},{3,4},{5,6},{2,1},{4,3},{6,5},{9,10},{11,12},{13,14},{10,9},... | collective-permute-start | bytes 98312 | tf_op jit(solution)/shard_map/ppermute | solution.py:267
  20.4 0.3 prep.1
  20.7 2.1 %collective-permute-done.2.chip_ref = bf16[4,32,128]{2,1,0:T(8,128)(2,1)S(1)} collective-permute-done((bf16[4,32,128]{2,1,0:T(8,128)(2,1)S(1)}, bf16[4,32,128]{2,1,0:T(8,128)(2,1)S(1)}, u32[]{:S(2)}, u32[]{:S(2)}) %collective-permute-start.2) | collective-permute-done | bytes 32800 | tf_op jit(solution)/shard_map/ppermute | solution.py:267
  22.8 1.9 %dynamics.1 = (f32[16,2,32,128]{3,2,1,0:T(8,128)S(1)}, f32[1,128]{1,0:T(1,128)S(1)}) custom-call(f32[16,32,128]{2,1,0:T(8,128)S(1)} %get-tuple-element.40.guess_ref, bf16[17,32,128]{2,1,0:T(8,128)(2,1)S(1)} %collective-permute-done.shift_ref, bf16[4,32,128]{2,1,0:T(8,128)(2,1)S(1)} %collective-permute-done.1.pair_ref, ...), custom_call_target="tpu_custom_call" | custom-call | tf_op jit(solution)/shard_map/dynamics/pallas_call | solution.py:271
  24.8 0.8 convert_element_type.287
  25.5 4.1 %all-to-all-start = ((f16[16,2,32,128]{3,2,1,0:T(8,128)(2,1)}), f16[16,2,32,128]{3,2,1,0:T(8,128)(2,1)S(1)}, u32[]{:S(2)}, u32[]{:S(2)}) async-start(f16[16,2,32,128]{3,2,1,0:T(8,128)(2,1)} %convert_element_type.287), calls=%async_computation | async-start | bytes 524288 | tf_op jit(solution)/shard_map/all_to_all | solution.py:289
  29.6 1.9 %collective-permute-start.3 = (f32[1,128]{1,0:T(1,128)S(1)}, f32[1,128]{1,0:T(1,128)S(1)}, u32[]{:S(2)}, u32[]{:S(2)}) collective-permute-start(f32[1,128]{1,0:T(1,128)S(1)} %get-tuple-element.49), channel_id=1, source_target_pairs={{0,1},{1,0},{2,3},{3,2},{4,5},{5,4},{6,7},{7,6},{8,9},{9,8},{10,11... | collective-permute-start | bytes 1544 | tf_op jit(solution)/shard_map/ppermute | solution.py:291
  31.6 1.1 %collective-permute-done.3 = f32[1,128]{1,0:T(1,128)S(1)} collective-permute-done((f32[1,128]{1,0:T(1,128)S(1)}, f32[1,128]{1,0:T(1,128)S(1)}, u32[]{:S(2)}, u32[]{:S(2)}) %collective-permute-start.3) | collective-permute-done | bytes 544 | tf_op jit(solution)/shard_map/ppermute | solution.py:291
  32.7 2.6 %collective-permute-start.4 = (f32[1,128]{1,0:T(1,128)S(1)}, f32[1,128]{1,0:T(1,128)S(1)}, u32[]{:S(2)}, u32[]{:S(2)}) collective-permute-start(f32[1,128]{1,0:T(1,128)S(1)} %add.130), channel_id=1, source_target_pairs={{0,2},{1,3},{2,0},{3,1},{4,6},{5,7},{6,4},{7,5},{8,10},{9,11},{10,... | collective-permute-start | bytes 1544 | tf_op jit(solution)/shard_map/ppermute | solution.py:291
  35.3 2.8 %collective-permute-done.4 = f32[1,128]{1,0:T(1,128)S(1)} collective-permute-done((f32[1,128]{1,0:T(1,128)S(1)}, f32[1,128]{1,0:T(1,128)S(1)}, u32[]{:S(2)}, u32[]{:S(2)}) %collective-permute-start.4) | collective-permute-done | bytes 544 | tf_op jit(solution)/shard_map/ppermute | solution.py:291
  38.1 2.0 %collective-permute-start.5 = (f32[1,128]{1,0:T(1,128)S(1)}, f32[1,128]{1,0:T(1,128)S(1)}, u32[]{:S(2)}, u32[]{:S(2)}) collective-permute-start(f32[1,128]{1,0:T(1,128)S(1)} %add.131), channel_id=1, source_target_pairs={{0,6},{1,7},{2,4},{3,5},{4,2},{5,3},{6,0},{7,1},{8,14},{9,15},{10,... | collective-permute-start | bytes 1544 | tf_op jit(solution)/shard_map/ppermute | solution.py:291
  40.2 4.6 %collective-permute-done.5 = f32[1,128]{1,0:T(1,128)S(1)} collective-permute-done((f32[1,128]{1,0:T(1,128)S(1)}, f32[1,128]{1,0:T(1,128)S(1)}, u32[]{:S(2)}, u32[]{:S(2)}) %collective-permute-start.5) | collective-permute-done | bytes 544 | tf_op jit(solution)/shard_map/ppermute | solution.py:291
  44.8 0.4 all-to-all-done
  45.5 9.7 %all_to_all.15 = f16[4,2,32,128]{3,2,1,0:T(8,128)(2,1)S(1)} all-to-all(f16[4,2,32,128]{3,2,1,0:T(8,128)(2,1)S(1)} %broadcast_in_dim.25), channel_id=1, replica_groups={{0,128,256,384},{8,136,264,392},{16,144,272,400},{24,152,280,408},{32,1..., dimensions={0} | all-to-all | bytes 131072 | tf_op jit(solution)/shard_map/all_to_all | solution.py:308
  55.3 0.7 fusion.2
  56.0 11.6 %all-to-all-start.2 = ((f16[16,32,128]{2,1,0:T(8,128)(2,1)}), f16[16,32,128]{2,1,0:T(8,128)(2,1)S(1)}, u32[]{:S(2)}, u32[]{:S(2)}) async-start(f16[16,32,128]{2,1,0:T(8,128)(2,1)} %fusion.2), calls=%async_computation.2 | async-start | bytes 262144 | tf_op jit(solution)/shard_map/all_to_all | solution.py:313
  67.5 3.8 %collective-permute-start.6 = (f32[1,128]{1,0:T(1,128)S(1)}, f32[1,128]{1,0:T(1,128)S(1)}, u32[]{:S(2)}, u32[]{:S(2)}) collective-permute-start(f32[1,128]{1,0:T(1,128)S(1)} %add.132), channel_id=1, source_target_pairs={{0,8},{8,16},{16,24},{24,32},{32,40},{40,48},{48,56},{56,64},{64,7... | collective-permute-start | bytes 1544 | tf_op jit(solution)/shard_map/ppermute | solution.py:314
  71.4 5.0 %collective-permute-done.6 = f32[1,128]{1,0:T(1,128)S(1)} collective-permute-done((f32[1,128]{1,0:T(1,128)S(1)}, f32[1,128]{1,0:T(1,128)S(1)}, u32[]{:S(2)}, u32[]{:S(2)}) %collective-permute-start.6) | collective-permute-done | bytes 544 | tf_op jit(solution)/shard_map/ppermute | solution.py:314
  76.3 0.6 reduce_sum.9
  77.6 3.1 %all-to-all-done.2 = f16[16,32,128]{2,1,0:T(8,128)(2,1)S(1)} async-done(((f16[16,32,128]{2,1,0:T(8,128)(2,1)}), f16[16,32,128]{2,1,0:T(8,128)(2,1)S(1)}, u32[]{:S(2)}, u32[]{:S(2)}) %all-to-all-start.2) | async-done | bytes 131104 | tf_op jit(solution)/shard_map/all_to_all | solution.py:313
  80.7 0.9 %copy.13 = f32[1,32,16,128]{3,2,1,0:T(8,128)} copy(f32[1,32,16,128]{3,1,2,0:T(8,128)S(1)} %convert_bitcast_fusion) | data formatting | bytes 524288
  (14 shorter events, 0.3 us)
Async XLA Ops:
  2.1 20.8 %collective-permute-start = (bf16[17,32,128]{2,1,0:T(8,128)(2,1)S(1)}, bf16[17,32,128]{2,1,0:T(8,128)(2,1)S(1)}, u32[]{:S(2)}, u32[]{:S(2)}) collective-permute-start(bf16[17,32,128]{2,1,0:T(8,128)(2,1)S(1)} %get-tuple-element.41), channel_id=1, source_target_pairs={{8,0},{16,8},{24,16},{32,24},{40,32},{48,40},{56,48},{64,56},{72,6... | collective-permute-start | bytes 417800 | tf_op jit(solution)/shard_map/ppermute | solution.py:266
  15.7 5.0 %collective-permute-start.1 = (bf16[4,32,128]{2,1,0:T(8,128)(2,1)S(1)}, bf16[4,32,128]{2,1,0:T(8,128)(2,1)S(1)}, u32[]{:S(2)}, u32[]{:S(2)}) collective-permute-start(bf16[4,32,128]{2,1,0:T(8,128)(2,1)S(1)} %get-tuple-element.42), channel_id=1, source_target_pairs={{0,1},{1,0},{2,3},{3,2},{4,5},{5,4},{6,7},{7,6},{8,9},{9,8},{10,11... | collective-permute-start | bytes 98312 | tf_op jit(solution)/shard_map/ppermute | solution.py:268
  17.6 5.2 %collective-permute-start.2 = (bf16[4,32,128]{2,1,0:T(8,128)(2,1)S(1)}, bf16[4,32,128]{2,1,0:T(8,128)(2,1)S(1)}, u32[]{:S(2)}, u32[]{:S(2)}) collective-permute-start(bf16[4,32,128]{2,1,0:T(8,128)(2,1)S(1)} %get-tuple-element.43), channel_id=1, source_target_pairs={{1,2},{3,4},{5,6},{2,1},{4,3},{6,5},{9,10},{11,12},{13,14},{10,9},... | collective-permute-start | bytes 98312 | tf_op jit(solution)/shard_map/ppermute | solution.py:267
  25.5 19.7 %all-to-all-start = ((f16[16,2,32,128]{3,2,1,0:T(8,128)(2,1)}), f16[16,2,32,128]{3,2,1,0:T(8,128)(2,1)S(1)}, u32[]{:S(2)}, u32[]{:S(2)}) async-start(f16[16,2,32,128]{3,2,1,0:T(8,128)(2,1)} %convert_element_type.287), calls=%async_computation | async-start | bytes 524288 | tf_op jit(solution)/shard_map/all_to_all | solution.py:289
  29.6 3.1 %collective-permute-start.3 = (f32[1,128]{1,0:T(1,128)S(1)}, f32[1,128]{1,0:T(1,128)S(1)}, u32[]{:S(2)}, u32[]{:S(2)}) collective-permute-start(f32[1,128]{1,0:T(1,128)S(1)} %get-tuple-element.49), channel_id=1, source_target_pairs={{0,1},{1,0},{2,3},{3,2},{4,5},{5,4},{6,7},{7,6},{8,9},{9,8},{10,11... | collective-permute-start | bytes 1544 | tf_op jit(solution)/shard_map/ppermute | solution.py:291
  32.7 5.5 %collective-permute-start.4 = (f32[1,128]{1,0:T(1,128)S(1)}, f32[1,128]{1,0:T(1,128)S(1)}, u32[]{:S(2)}, u32[]{:S(2)}) collective-permute-start(f32[1,128]{1,0:T(1,128)S(1)} %add.130), channel_id=1, source_target_pairs={{0,2},{1,3},{2,0},{3,1},{4,6},{5,7},{6,4},{7,5},{8,10},{9,11},{10,... | collective-permute-start | bytes 1544 | tf_op jit(solution)/shard_map/ppermute | solution.py:291
  38.1 6.7 %collective-permute-start.5 = (f32[1,128]{1,0:T(1,128)S(1)}, f32[1,128]{1,0:T(1,128)S(1)}, u32[]{:S(2)}, u32[]{:S(2)}) collective-permute-start(f32[1,128]{1,0:T(1,128)S(1)} %add.131), channel_id=1, source_target_pairs={{0,6},{1,7},{2,4},{3,5},{4,2},{5,3},{6,0},{7,1},{8,14},{9,15},{10,... | collective-permute-start | bytes 1544 | tf_op jit(solution)/shard_map/ppermute | solution.py:291
  56.0 24.7 %all-to-all-start.2 = ((f16[16,32,128]{2,1,0:T(8,128)(2,1)}), f16[16,32,128]{2,1,0:T(8,128)(2,1)S(1)}, u32[]{:S(2)}, u32[]{:S(2)}) async-start(f16[16,32,128]{2,1,0:T(8,128)(2,1)} %fusion.2), calls=%async_computation.2 | async-start | bytes 262144 | tf_op jit(solution)/shard_map/all_to_all | solution.py:313
  67.5 8.8 %collective-permute-start.6 = (f32[1,128]{1,0:T(1,128)S(1)}, f32[1,128]{1,0:T(1,128)S(1)}, u32[]{:S(2)}, u32[]{:S(2)}) collective-permute-start(f32[1,128]{1,0:T(1,128)S(1)} %add.132), channel_id=1, source_target_pairs={{0,8},{8,16},{16,24},{24,32},{32,40},{40,48},{48,56},{56,64},{64,7... | collective-permute-start | bytes 1544 | tf_op jit(solution)/shard_map/ppermute | solution.py:314
